TPU v7x, 32 devices: a whole 2x2x4 slice. The times are simulated.
32 devices in a mesh: groups: 2 (over y), cells: 4 (over z), sect: 2 (over x), lev: 2 (over core).
Axes of the slice: x: 2, y: 2, z: 4, core: 2. Of those that a mesh axis runs over, the one named last changes fastest.
Arguments:
- spectrum: bfloat16 [1152, 32, 256], P(('cells', 'lev'), 'groups', 'sect'), parts along dimension 1, may hold values from -6 to 6
- courant_x: float32 [1152], P(('cells', 'lev')), may hold values from -0.45 to 0.45
- courant_y: float32 [1152], P(('cells', 'lev')), may hold values from -0.45 to 0.45
- growth: float32 [1152], replicated, may hold values from 0.5 to 2
- quartet: bfloat16 [1152, 1152], replicated, may hold values from -0.1875 to 0.1875
- coupler: bfloat16 [128, 1152], replicated, may hold values from -0.1875 to 0.1875
- atmosphere: float32 [64, 32, 256], P('lev', ('groups', 'cells'), 'sect'), parts along dimension 1, may hold values from -6 to 6
- ocean_state: float32 [64, 32, 256], P('lev', ('groups', 'cells'), 'sect'), parts along dimension 1, may hold values from -6 to 6
- sea_mask: int32 [32, 256], P(('groups', 'cells'), 'sect'), parts along dimension 0, may hold values 0 or 1
Outputs:
- spectrum_out: bfloat16 [1152, 32, 256], P(('cells', 'lev'), 'groups', 'sect'), parts along dimension 1
- atmosphere_out: float32 [64, 32, 256], P('lev', ('groups', 'cells'), 'sect'), parts along dimension 1
- ocean_out: float32 [64, 32, 256], P('lev', ('groups', 'cells'), 'sect'), parts along dimension 1
There are 2 independent parts, one for each index of `groups`. A program takes and returns all parts, laid end to end along the dimension named above; an argument that names none is the same for every part. Nothing has to cross between parts.
Inputs may be any that keep to these rules, and one draw needn't show every extreme that they name: `sea_mask`: 1 marks a sea cell, 0 a land cell.
All inputs are finite; a program needn't handle non-finite values. No bound on the sum of `sea_mask` on one device may be relied on, other than what follows from the above.
Results may differ from a plain program's by a relative error of at most 0.0062.
Values may be sent and summed in bfloat16 or wider, within the bound.
A program may use at most 64 MiB of HBM per device.

v0:
```python
import functools

import jax
import jax.numpy as jnp
from jax import lax
from jax.experimental import pallas as pl
from jax.experimental.pallas import tpu as pltpu
from jax.sharding import PartitionSpec as P

NSTEP = 2
LANES = 128
F32 = jnp.float32
BF16 = jnp.bfloat16


def from_root(block, axis, source):
    block = jnp.where(lax.axis_index(axis) == source, block, jnp.zeros_like(block))
    return lax.psum(block, axis)


def extended_2(block, sides, width, periodic):
    for axis, dim in sides:
        count = lax.axis_size(axis)
        forward = [(i, i + 1) for i in range(count - 1)]
        if periodic:
            forward.append((count - 1, 0))
        backward = [(target, source) for source, target in forward]
        low = lax.ppermute(
            lax.slice_in_dim(block, block.shape[dim] - width, None, axis=dim), axis, forward
        )
        high = lax.ppermute(lax.slice_in_dim(block, 0, width, axis=dim), axis, backward)
        block = jnp.concatenate([low, block, high], axis=dim)
    return block


def upwind(values, courant, before, after):
    return jnp.maximum(courant, 0.0) * (values - before) + jnp.minimum(courant, 0.0) * (
        after - values
    )


def on_device(
    spectrum, courant_x, courant_y, growth, quartet, coupler, atmosphere, ocean_state, sea_mask
):
    cell_tiles = lax.axis_size("cells")
    lev_parts = lax.axis_size("lev")
    blocks = cell_tiles * lev_parts
    comps_own, rows_all, row_width = spectrum.shape
    total_comps = comps_own * blocks
    cell_rows = rows_all // blocks
    level_count = coupler.shape[0] // 2
    row_start = lax.axis_index("lev") * cell_rows
    shift_x = courant_x[:, None, None]
    shift_y = courant_y[:, None, None]
    sea_rows = (
        lax.dynamic_slice_in_dim(sea_mask, row_start, cell_rows, 0)
        .astype(jnp.float32)
        .reshape(1, cell_rows * row_width)
    )
    growth_column = growth[:, None]
    forcing_sign = jnp.array([-0.3, 0.3], jnp.float32)[:, None, None, None]
    state = jnp.stack([atmosphere, ocean_state])
    energy = spectrum
    for counter in range(NSTEP):
        surface = from_root(state[:, 0], "lev", 0)
        surface_wind = surface[0] - surface[1]
        wind_rows = lax.dynamic_slice_in_dim(
            surface_wind * surface_wind, row_start, cell_rows, 0
        ).reshape(1, cell_rows * row_width)
        padded = extended_2(energy, (("sect", 2),), 1, True)
        values = padded[:, :, 1:-1].astype(jnp.float32)
        west_side = padded[:, :, :-2].astype(jnp.float32)
        east_side = padded[:, :, 2:].astype(jnp.float32)
        moved = values - upwind(values, shift_x, west_side, east_side)
        moved = moved - upwind(
            values, shift_y, jnp.roll(values, 1, axis=1), jnp.roll(values, -1, axis=1)
        )
        advected = moved.astype(jnp.bfloat16)
        pieces = advected.reshape(1, comps_own, blocks, cell_rows, row_width)
        on_cells = lax.all_to_all(pieces, ("cells", "lev"), split_axis=2, concat_axis=0, tiled=True)
        on_cells = on_cells.reshape(total_comps, cell_rows * row_width)
        cell_values = on_cells.astype(jnp.float32)
        paired = jnp.dot(quartet, on_cells, preferred_element_type=jnp.float32)
        squared = (cell_values * cell_values).astype(jnp.bfloat16)
        quad_square = jnp.dot(quartet, squared, preferred_element_type=jnp.float32)
        fresh = (
            cell_values
            + 0.3 * (cell_values * paired - quad_square)
            + 0.1 * growth_column * wind_rows
        ) / (1.0 + 0.1 * cell_values * cell_values)
        fresh = (fresh * sea_rows).astype(jnp.bfloat16)
        profile = jnp.dot(coupler, fresh, preferred_element_type=jnp.float32).reshape(
            2, level_count, cell_rows, row_width
        )
        forcing = lax.all_to_all(profile, "lev", split_axis=1, concat_axis=2, tiled=True)
        returned = fresh.reshape(blocks, comps_own, 1, cell_rows, row_width)
        returned = lax.all_to_all(
            returned, ("cells", "lev"), split_axis=0, concat_axis=2, tiled=True
        )
        energy = returned.reshape(comps_own, rows_all, row_width)
        extended = extended_2(state, (("lev", 1), ("cells", 2), ("sect", 3)), 1, False)
        middle = extended[:, 1:-1, 1:-1, 1:-1]
        lateral = (
            extended[:, 1:-1, 2:, 1:-1]
            + extended[:, 1:-1, :-2, 1:-1]
            + extended[:, 1:-1, 1:-1, 2:]
            + extended[:, 1:-1, 1:-1, :-2]
            - 4.0 * middle
        )
        upright = extended[:, 2:, 1:-1, 1:-1] + extended[:, :-2, 1:-1, 1:-1] - 2.0 * middle
        state = middle + 0.1 * lateral + 0.1 * upright + forcing_sign * forcing
    return (energy, state[0], state[1])


def column_of(row):
    n = row.shape[1]
    down = lax.broadcasted_iota(jnp.int32, (n, n), 0)
    across = lax.broadcasted_iota(jnp.int32, (n, n), 1)
    return jnp.sum(jnp.where(down == across, row, 0.0), axis=1, keepdims=True)


def swap_groups(vectors, seg):
    count = len(vectors)
    width = vectors[0].shape[1]
    group = lax.broadcasted_iota(jnp.int32, vectors[0].shape, 1) // seg
    dist = count // 2
    vectors = list(vectors)
    while dist:
        even = (group // dist) % 2 == 0
        for i in range(count):
            if (i // dist) % 2 == 0:
                x, y = vectors[i], vectors[i + dist]
                if 2 * dist * seg == width:
                    moved = pltpu.roll(jnp.where(even, y, x), dist * seg, 1)
                    vectors[i], vectors[i + dist] = jnp.where(even, x, moved), jnp.where(even, moved, y)
                else:
                    vectors[i] = jnp.where(even, x, pltpu.roll(y, dist * seg, 1))
                    vectors[i + dist] = jnp.where(even, pltpu.roll(x, width - dist * seg, 1), y)
        dist //= 2
    return vectors


def fused_kernel(
    cell_tiles, lev_parts, sect_tiles,
    spec_hbm, cx_hbm, cy_hbm, growth_hbm, quartet_hbm, coupler_hbm, atm_hbm, oce_hbm, sea_hbm,
    ret, fin,
    spec_v, cx_v, cy_v, growth_v, quartet_v, coupler_v, col_in, sea_v,
    flat, rows_v, send_f, cell_f, cell_s, cx_all, cy_all, cxb, cyb, grow_b,
    edge_send, edge_recv, e1, e2,
    swap_send, st_in, sea_send, sea_in, outer, inner, st0, st1, st2, st_edge_send, st_edge_recv, st_back,
    in_sem, own_sem, f_send, f_recv, c_send, c_recv,
    edge_ss, edge_rs, swap_ss, swap_rs, sea_ss, sea_rs, back_ss, back_rs, ste_ss, ste_rs,
    ret_ss, ret_rs,
):
    blocks = cell_tiles * lev_parts
    comps, rows, width = spec_v.shape
    lines = rows // blocks
    lown = col_in.shape[1]
    tile_rows = col_in.shape[2]
    levels = lown * lev_parts
    seg = width // blocks
    mid = width // 2
    mine_c = lax.axis_index("cells")
    mine_l = lax.axis_index("lev")
    mine_x = lax.axis_index("sect")
    me = mine_c * lev_parts + mine_l
    turned = lax.rem(mine_x, 2) == 1
    side = lax.div(mine_c, cell_tiles // 2)

    def tile_of(b):
        return jnp.where(turned, blocks - 1 - b, b)

    def mirrored(b):
        return jnp.where(side == 1, blocks - 1 - b, b)

    def block_id(b):
        return {"cells": lax.div(b, lev_parts), "lev": lax.rem(b, lev_parts)}

    spot = tile_of(me)
    inside = mirrored(me)
    west = {"sect": lax.rem(mine_x + sect_tiles - 1, sect_tiles)}
    east = {"sect": lax.rem(mine_x + 1, sect_tiles)}
    near_west = {
        **block_id(jnp.where(spot == 0, me, tile_of(spot - 1))),
        "sect": jnp.where(spot == 0, west["sect"], mine_x),
    }
    near_east = {
        **block_id(jnp.where(spot == blocks - 1, me, tile_of(spot + 1))),
        "sect": jnp.where(spot == blocks - 1, east["sect"], mine_x),
    }
    half = blocks // 2
    odd = lax.rem(inside, 2)
    across = [mirrored(blocks - 1 - i + (1 - 2 * (i % 2)) * -odd) for i in range(half)]
    mate = (1 - lax.div(inside, lev_parts)) * lev_parts
    mates = [mirrored(mate + k) for k in range(lev_parts)]
    order = across + mates + [mirrored(inside + 1 - 2 * odd)]

    def part(b):
        return pl.ds(pl.multiple_of(b * comps, 16), comps)

    def remote(src, dst, ss, rs, where):
        return pltpu.make_async_remote_copy(
            src_ref=src, dst_ref=dst, send_sem=ss, recv_sem=rs,
            device_id=where, device_id_type=pl.DeviceIdType.MESH,
        )

    loads = [
        pltpu.make_async_copy(a, b, in_sem.at[i])
        for i, (a, b) in enumerate([
            (spec_hbm, spec_v), (cx_hbm, cx_v), (cy_hbm, cy_v),
            (atm_hbm, col_in.at[0]), (oce_hbm, col_in.at[1]), (sea_hbm, sea_v),
            (growth_hbm, growth_v), (coupler_hbm, coupler_v), (quartet_hbm, quartet_v),
        ])
    ]
    for load in loads:
        load.start()

    barrier = pltpu.get_barrier_semaphore()
    for d in range(1, blocks):
        pl.semaphore_signal(barrier, inc=1, device_id=block_id(lax.rem(me + d, blocks)),
                            device_id_type=pl.DeviceIdType.MESH)
    for side_id in (west, east, near_west, near_east):
        pl.semaphore_signal(barrier, inc=1, device_id=side_id,
                            device_id_type=pl.DeviceIdType.MESH)

    lane = lax.broadcasted_iota(jnp.int32, (comps, width), 1)
    loads[0].wait()
    flat[...] = spec_v[...].astype(F32).reshape(comps * rows, width)
    first = jnp.zeros((comps, width), F32)
    last = jnp.zeros((comps, width), F32)
    for r in range(rows):
        v = flat[pl.ds(r, comps, stride=rows), :]
        rows_v[r] = v
        place = (r % blocks) * seg + r // blocks
        first = jnp.where(lane == place, pltpu.roll(v, place, 1), first)
        last = jnp.where(lane == place, pltpu.roll(v, (place + 1) % width, 1), last)
    edge_send[0, 0] = first.astype(BF16)
    edge_send[0, 1] = last.astype(BF16)

    pl.semaphore_wait(barrier, blocks + 3)
    pending = []

    def send_edges(step):
        copies = [
            remote(edge_send.at[step, i], edge_recv.at[step, i],
                   edge_ss.at[step, i], edge_rs.at[step, i], where)
            for i, where in enumerate((west, east) if step == 0 else (near_west, near_east))
        ]
        for copy in copies:
            copy.start()
        pending.extend(copies)
        return copies

    edges = send_edges(0)

    loads[1].wait()
    loads[2].wait()
    for d, b in enumerate(order):
        for i, (src, dst) in enumerate(((cx_v, cx_all), (cy_v, cy_all))):
            copy = remote(src, dst.at[me], c_send.at[i, d], c_recv.at[i, me], block_id(b))
            copy.start()
            pending.append(copy)

    my_levels = pl.ds(pl.multiple_of(mine_l * lown, 16), lown)

    def state_in(b):
        return remote(swap_send.at[tile_of(b)], st_in.at[mine_c, my_levels, :], swap_ss.at[b],
                      swap_rs.at[mine_c, mine_l], block_id(b))

    def sea_over(c):
        return remote(sea_send.at[tile_of(c * lev_parts + mine_l)], sea_in.at[mine_c], sea_ss.at[c],
                      sea_rs.at[mine_c], {"cells": c})

    def send_state_in():
        loads[3].wait()
        loads[4].wait()
        loads[5].wait()
        groups = [col_in[f, :, r, :] for f in range(2) for r in range(tile_rows)]
        for t, line in enumerate(swap_groups(groups, seg)):
            swap_send[t] = line.astype(BF16)
        groups = [jnp.broadcast_to(sea_v[r:r + 1, :].astype(F32), (8, width)) for r in range(tile_rows)]
        for t, line in enumerate(swap_groups(groups + [jnp.zeros((8, width), F32)] * tile_rows, seg)):
            sea_send[t] = line[0:1]
        for b in order:
            state_in(b).start()
        for dc in range(1, cell_tiles):
            sea_over(lax.rem(mine_c + dc, cell_tiles)).start()
        st_in[mine_c, my_levels, :] = swap_send[spot]
        sea_in[mine_c] = sea_send[spot]

    def halves(c):
        return jnp.maximum(c, 0.0), jnp.maximum(-c, 0.0)

    cxb[part(me), :] = jnp.broadcast_to(column_of(cx_v[...]), (comps, width))
    cyb[part(me), :] = jnp.broadcast_to(column_of(cy_v[...]), (comps, width))

    def send_line(b, h):
        t = tile_of(b)
        cut = slice(h * width, (h + 1) * width)

        @pl.when(b != me)
        def _():
            remote(send_f.at[t, h], cell_f.at[part(me), cut], f_send.at[b, h], f_recv.at[me, h],
                   block_id(b)).start()

        @pl.when(b == me)
        def _():
            cell_f[part(me), cut] = send_f[spot, h]

    chunk = 16
    small = lax.broadcasted_iota(jnp.int32, (chunk, width), 1)
    at_rim = inside < lev_parts

    for h in range(lines):
        for k in range(0, comps, chunk):
            own = pl.ds(pl.multiple_of(me * comps + k, 16), chunk)
            cx = cxb[own, :]
            cy = cyb[own, :]
            px, mx = halves(cx)
            py, my = halves(cy)
            keep = 1.0 - jnp.abs(cx) - jnp.abs(cy)
            groups = []
            for g in range(blocks):
                row = h * blocks + g
                v = rows_v[row, k:k + chunk]
                to_west = jnp.where(small == 0, 0.0, pltpu.roll(v, 1, 1))
                to_east = jnp.where(small == width - 1, 0.0, pltpu.roll(v, width - 1, 1))
                groups.append(
                    v * keep + px * to_west + mx * to_east
                    + py * rows_v[(row + rows - 1) % rows, k:k + chunk] + my * rows_v[(row + 1) % rows, k:k + chunk]
                )
            for t, line in enumerate(swap_groups(groups, seg)):
                if 0 < t < blocks - 1:
                    send_f[t, h, k:k + chunk] = line.astype(BF16)
                else:
                    outer[min(t, 1), h, k:k + chunk] = line
        for i in range(blocks - 2, half - 1, -1):
            send_line(mirrored(i), h)
        send_line(mirrored(1), h)

        @pl.when(jnp.logical_not(at_rim))
        def _():
            for i in range(2, half):
                send_line(mirrored(i), h)
    send_state_in()
    for copy in edges:
        copy.wait_recv()
    for k in range(0, comps, chunk):
        cx = cxb[pl.ds(pl.multiple_of(me * comps + k, 16), chunk), :]
        px, mx = halves(cx)
        from_east = edge_recv[0, 0, k:k + chunk].astype(F32)
        from_west = edge_recv[0, 1, k:k + chunk].astype(F32)
        for h in range(lines):
            west_part = jnp.where(small % seg == 0, pltpu.roll(from_west, (width - h) % width, 1), 0.0)
            east_part = jnp.where(small % seg == seg - 1, pltpu.roll(from_east, seg - 1 - h, 1), 0.0)
            send_f[0, h, k:k + chunk] = (outer[0, h, k:k + chunk] + px * west_part).astype(BF16)
            send_f[blocks - 1, h, k:k + chunk] = (outer[1, h, k:k + chunk] + mx * east_part).astype(BF16)
    for i in (blocks - 1, 0):
        for h in range(lines):
            send_line(mirrored(i), h)

    @pl.when(at_rim)
    def _():
        for i in range(2, half):
            for h in range(lines):
                send_line(mirrored(i), h)

    level_id = lax.broadcasted_iota(jnp.int32, (levels, width), 0)
    level_lane = lax.broadcasted_iota(jnp.int32, (levels, width), 1)
    place = level_lane % seg
    folds = seg // (2 * lines)
    depth = levels // folds
    fold_place = place[:depth]

    def fold_slots():
        for f in range(2):
            for r in range(lines):
                for q in range(folds):
                    yield f, r, slice(q * depth, (q + 1) * depth), (q * 2 + f) * lines + r

    def send_state(state, step):
        west_pack = jnp.zeros((depth, width), F32)
        east_pack = jnp.zeros((depth, width), F32)
        for f, r, cut, slot in fold_slots():
            v = state[f, r, cut]
            west_pack = jnp.where(fold_place == slot, pltpu.roll(v, slot, 1), west_pack)
            east_pack = jnp.where(fold_place == slot, pltpu.roll(v, (slot + 1 - seg) % width, 1), east_pack)
        st_edge_send[step, 0] = west_pack
        st_edge_send[step, 1] = east_pack
        copies = []
        for i, where in enumerate((near_west, near_east)):
            copies.append(remote(st_edge_send.at[step, i], st_edge_recv.at[step, i],
                                 ste_ss.at[step, i], ste_rs.at[step, i], where))
        for copy in copies:
            copy.start()
        pending.extend(copies)
        return copies

    def update(state, new, step, profile):
        rim_west = (mine_x == 0) & (spot == 0)
        rim_east = (mine_x == sect_tiles - 1) & (spot == blocks - 1)
        west_pack = jnp.where(rim_west, 0.0, st_edge_recv[step, 1])
        east_pack = jnp.where(rim_east, 0.0, st_edge_recv[step, 0])
        sides = {}
        for f, r, cut, slot in fold_slots():
            sides.setdefault((f, r), []).append((
                pltpu.roll(west_pack, (width - slot) % width, 1),
                pltpu.roll(east_pack, (width + seg - 1 - slot) % width, 1),
            ))
        for f in range(2):
            factor = -0.3 if f == 0 else 0.3
            for r in range(lines):
                v = state[f, r]
                w = jnp.where(place == 0, jnp.concatenate([x for x, _ in sides[f, r]]), pltpu.roll(v, 1, 1))
                e = jnp.where(place == seg - 1, jnp.concatenate([x for _, x in sides[f, r]]),
                              pltpu.roll(v, width - 1, 1))
                n = 0.0 if r == 0 else state[f, r - 1]
                s = 0.0 if r == lines - 1 else state[f, r + 1]
                n = pltpu.roll(jnp.where(level_lane >= width - seg, n, v), seg, 1)
                s = pltpu.roll(jnp.where(level_lane < seg, s, v), width - seg, 1)
                below = jnp.where(level_id == 0, 0.0, pltpu.roll(v, 1, 0))
                above = jnp.where(level_id == levels - 1, 0.0, pltpu.roll(v, levels - 1, 0))
                g = profile[f * levels:(f + 1) * levels, r * width:(r + 1) * width]
                new[f, r] = (v + 0.1 * (n + s + w + e - 4.0 * v)
                             + 0.1 * (above + below - 2.0 * v) + factor * g)

    loads[6].wait()
    for t in range(growth_v.shape[0] // LANES):
        column = column_of(growth_v[t * LANES:(t + 1) * LANES].reshape(1, LANES))
        grow_b[t * LANES:(t + 1) * LANES, :] = jnp.broadcast_to(0.1 * column, (LANES, width))

    def wind(state):
        out = []
        for r in range(lines):
            diff = state[0, r, 0:1, :] - state[1, r, 0:1, :]
            out.append(diff * diff)
        return out

    def fresh_part(b, wind_rows, target):
        weights = quartet_v[part(b), :]
        pair = jnp.dot(weights, cell_f[...], preferred_element_type=F32)
        quad = jnp.dot(weights, cell_s[...], preferred_element_type=F32)
        outs = []
        for r in range(lines):
            cut = slice(r * width, (r + 1) * width)
            f = cell_f[part(b), cut].astype(F32)
            top = f + 0.3 * (f * pair[:, cut] - quad[:, cut]) + grow_b[part(b), :] * wind_rows[r]
            out = (sea[r] * (top / (1.0 + 0.1 * (f * f)))).astype(BF16)
            target[part(b), cut] = out
            outs.append(out)
        return outs

    def square(b):
        f = cell_f[part(b), :].astype(F32)
        cell_s[part(b), :] = (f * f).astype(BF16)

    square(me)
    for b in order[::-1]:
        for i, dst in enumerate((cx_all, cy_all)):
            remote(dst.at[b], dst.at[b], c_send.at[i, 0], c_recv.at[i, b], block_id(b)).wait_recv()
        cxb[part(b), :] = jnp.broadcast_to(column_of(cx_all[b]), (comps, width))
        cyb[part(b), :] = jnp.broadcast_to(column_of(cy_all[b]), (comps, width))
    for b in order[::-1]:
        c = lax.div(b, lev_parts)
        core = lax.rem(b, lev_parts)
        there = st_in.at[c, pl.ds(pl.multiple_of(core * lown, 16), lown), :]
        remote(there, there, swap_ss.at[0], swap_rs.at[c, core], block_id(b)).wait_recv()
    for dc in range(1, cell_tiles):
        c = lax.rem(mine_c + dc, cell_tiles)
        remote(sea_in.at[c], sea_in.at[c], sea_ss.at[0], sea_rs.at[c], {"cells": c}).wait_recv()

    wide_lane = lax.broadcasted_iota(jnp.int32, (8, width), 1)
    sea = []
    for h in range(lines):
        low = st_in[2 * h].astype(F32)
        high = st_in[2 * h + 1].astype(F32)
        st0[0, h] = jnp.where(level_lane < mid, low, pltpu.roll(high, mid, 1))
        st0[1, h] = jnp.where(level_lane < mid, pltpu.roll(low, mid, 1), high)
        low = jnp.broadcast_to(sea_in[2 * h], (8, width))
        high = jnp.broadcast_to(sea_in[2 * h + 1], (8, width))
        sea.append(jnp.where(wide_lane < mid, low, pltpu.roll(high, mid, 1))[0:1])
    state_copies = send_state(st0, 0)

    loads[7].wait()
    loads[8].wait()
    for b in order[::-1]:
        for h in range(lines):
            cut = slice(h * width, (h + 1) * width)
            remote(cell_f.at[part(b), cut], cell_f.at[part(b), cut], f_send.at[0, 0], f_recv.at[b, h],
                   block_id(b)).wait_recv()
        square(b)

    wind_rows = wind(st0)
    first = jnp.zeros((comps, width), F32)
    last = jnp.zeros((comps, width), F32)
    for b in range(blocks):
        outs = fresh_part(b, wind_rows, e1)
        for r in range(lines):
            slot = b * lines + r
            v = outs[r].astype(F32)
            first = jnp.where(lane % seg == slot, pltpu.roll(v, slot, 1), first)
            last = jnp.where(lane % seg == slot, pltpu.roll(v, (slot + 1 - seg) % width, 1), last)
    edge_send[1, 0] = first.astype(BF16)
    edge_send[1, 1] = last.astype(BF16)
    edges = send_edges(1)

    west_rim = lane % seg == 0
    east_rim = lane % seg == seg - 1
    for b in range(blocks):
        cx = cxb[part(b), :]
        cy = cyb[part(b), :]
        px, mx = halves(cx)
        py, my = halves(cy)
        keep = 1.0 - jnp.abs(cx) - jnp.abs(cy)
        field = [e1[part(b), r * width:(r + 1) * width].astype(F32) for r in range(lines)]
        for r in range(lines):
            v = field[r]
            north = pltpu.roll(jnp.where(lane >= width - seg, field[r - 1], v), seg, 1)
            south = pltpu.roll(jnp.where(lane < seg, field[(r + 1) % lines], v), width - seg, 1)
            to_west = jnp.where(west_rim, 0.0, pltpu.roll(v, 1, 1))
            to_east = jnp.where(east_rim, 0.0, pltpu.roll(v, width - 1, 1))
            inner[part(b), r * width:(r + 1) * width] = (
                v * keep + px * to_west + mx * to_east + py * north + my * south
            )

    for copy in state_copies:
        copy.wait_recv()
    update(st0, st1, 0, jnp.dot(coupler_v[...], e1[...], preferred_element_type=F32))
    state_copies = send_state(st1, 1)
    wind_rows = wind(st1)

    for copy in edges:
        copy.wait_recv()
    from_east = edge_recv[1, 0].astype(F32)
    from_west = edge_recv[1, 1].astype(F32)
    for b in range(blocks):
        px, mx = halves(cxb[part(b), :])
        for r in range(lines):
            slot = b * lines + r
            cut = slice(r * width, (r + 1) * width)
            beside = jnp.where(
                west_rim, px * pltpu.roll(from_west, (width - slot) % width, 1),
                mx * pltpu.roll(from_east, (width + seg - 1 - slot) % width, 1),
            )
            out = (inner[part(b), cut] + jnp.where(west_rim | east_rim, beside, 0.0)).astype(BF16)
            cell_f[part(b), cut] = out
            wide = out.astype(F32)
            cell_s[part(b), cut] = (wide * wide).astype(BF16)

    for d, b in enumerate(order + [me]):
        fresh_part(b, wind_rows, e2)
        if d < blocks - 1:
            copy = remote(e2.at[part(b), :], ret.at[spot], ret_ss.at[d], ret_rs.at[spot], block_id(b))
            copy.start()
            pending.append(copy)

    for copy in state_copies:
        copy.wait_recv()
    update(st1, st2, 1, jnp.dot(coupler_v[...], e2[...], preferred_element_type=F32))
    for h in range(lines):
        atm = st2[0, h]
        oce = st2[1, h]
        st_back[2 * h] = jnp.where(level_lane < mid, atm, pltpu.roll(oce, mid, 1)).astype(BF16)
        st_back[2 * h + 1] = jnp.where(level_lane < mid, pltpu.roll(atm, mid, 1), oce).astype(BF16)

    for d, b in enumerate(order):
        c = lax.div(b, lev_parts)
        core = lax.rem(b, lev_parts)
        copy = remote(st_back.at[c, pl.ds(pl.multiple_of(core * lown, 16), lown), :], fin.at[spot], back_ss.at[d],
                      back_rs.at[spot], block_id(b))
        copy.start()
        pending.append(copy)
    stores = [
        pltpu.make_async_copy(st_back.at[mine_c, my_levels, :], fin.at[spot], own_sem.at[0]),
        pltpu.make_async_copy(e2.at[part(me), :], ret.at[spot], own_sem.at[1]),
    ]
    for store in stores:
        store.start()
    for b in order[::-1]:
        t = tile_of(b)
        remote(e2.at[part(b), :], ret.at[t], ret_ss.at[0], ret_rs.at[t], block_id(b)).wait_recv()
    for b in order[::-1]:
        t = tile_of(b)
        remote(fin.at[t], fin.at[t], back_ss.at[0], back_rs.at[t], block_id(b)).wait_recv()

    for b in order:
        state_in(b).wait_send()
        for h in range(lines):
            remote(send_f.at[tile_of(b), h], send_f.at[tile_of(b), h], f_send.at[b, h], f_recv.at[0, 0],
                   block_id(b)).wait_send()
    for dc in range(1, cell_tiles):
        sea_over(lax.rem(mine_c + dc, cell_tiles)).wait_send()
    for copy in pending:
        copy.wait_send()
    for store in stores:
        store.wait()


def unpack_kernel(ret, fin, spec_out, atm_out, oce_out, ret_v, fin_v, atm_v, oce_v, flat, spec_v, in_sem, out_sem):
    blocks, comps, cells = ret_v.shape
    rows, width = spec_v.shape[1:]
    lines = cells // width
    seg = width // blocks
    tile_rows = atm_v.shape[1]
    loads = [pltpu.make_async_copy(ret.at[b], ret_v.at[b], in_sem.at[b]) for b in range(blocks)]
    loads.append(pltpu.make_async_copy(fin, fin_v, in_sem.at[blocks]))
    for load in loads:
        load.start()
    loads[-1].wait()
    stores = []
    groups = swap_groups([fin_v[t].astype(F32) for t in range(blocks)], seg)
    for f, (target, out) in enumerate(((atm_v, atm_out), (oce_v, oce_out))):
        for r in range(tile_rows):
            target[:, r, :] = groups[f * tile_rows + r]
        stores.append(pltpu.make_async_copy(target, out, out_sem.at[f]))
        stores[-1].start()
    for load in loads[:-1]:
        load.wait()
    pieces = 3 if comps % 48 == 0 else 1
    size = comps // pieces
    for p in range(pieces):
        for k in range(p * size, (p + 1) * size, 16):
            for h in range(lines):
                groups = swap_groups([
                    ret_v[t, k:k + 16, h * width:(h + 1) * width].astype(F32) for t in range(blocks)
                ], seg)
                for g, line in enumerate(groups):
                    flat[pl.ds(k * rows + h * blocks + g, 16, stride=rows), :] = line
            spec_v[k:k + 16] = flat[k * rows:(k + 16) * rows, :].reshape(16, rows, width).astype(BF16)
        cut = pl.ds(p * size, size)
        stores.append(pltpu.make_async_copy(spec_v.at[cut], spec_out.at[cut], out_sem.at[2 + p]))
        stores[-1].start()
    for store in stores:
        store.wait()


def fused(
    spectrum, courant_x, courant_y, growth, quartet, coupler, atmosphere, ocean_state, sea_mask
):
    cell_tiles = lax.axis_size("cells")
    lev_parts = lax.axis_size("lev")
    sect_tiles = lax.axis_size("sect")
    blocks = cell_tiles * lev_parts
    comps, rows, width = spectrum.shape
    total = comps * blocks
    lines = rows // blocks
    lown, tile_rows, _ = atmosphere.shape
    levels = lown * lev_parts
    cells = lines * width
    depth = levels // (width // blocks // (2 * lines))
    v = pltpu.VMEM
    dma = pltpu.SemaphoreType.DMA
    scratch = [
        v((comps, rows, width), BF16), v((1, comps), F32), v((1, comps), F32),
        v((total,), F32), v((total, total), BF16), v(coupler.shape, BF16),
        v((2, lown, tile_rows, width), F32), v(sea_mask.shape, jnp.int32),
        v((comps * rows, width), F32), v((rows, comps, width), F32),
        v((blocks, lines, comps, width), BF16), v((total, cells), BF16), v((total, cells), BF16),
        v((blocks, 1, comps), F32), v((blocks, 1, comps), F32),
        v((total, width), F32), v((total, width), F32), v((total, width), F32),
        v((NSTEP, 2, comps, width), BF16), v((NSTEP, 2, comps, width), BF16),
        v((total, cells), BF16), v((total, cells), BF16),
        v((blocks, lown, width), BF16), v((cell_tiles, levels, width), BF16),
        v((blocks, 1, width), F32), v((cell_tiles, 1, width), F32),
        v((2, lines, comps, width), F32), v((total, cells), F32),
        v((2, lines, levels, width), F32), v((2, lines, levels, width), F32),
        v((2, lines, levels, width), F32),
        v((NSTEP, 2, depth, width), F32), v((NSTEP, 2, depth, width), F32),
        v((cell_tiles, levels, width), BF16),
        dma((9,)), dma((2,)), dma((blocks, lines)), dma((blocks, lines)),
        dma((2, blocks)), dma((2, blocks)),
        dma((NSTEP, 2)), dma((NSTEP, 2)),
        dma((blocks,)), dma((cell_tiles, lev_parts)), dma((cell_tiles,)), dma((cell_tiles,)),
        dma((blocks,)), dma((blocks,)),
        dma((NSTEP, 2)), dma((NSTEP, 2)),
        dma((blocks,)), dma((blocks,)),
    ]
    anywhere = pl.BlockSpec(memory_space=pltpu.HBM)
    column = jax.ShapeDtypeStruct(atmosphere.shape, F32)
    packed = pl.pallas_call(
        functools.partial(fused_kernel, cell_tiles, lev_parts, sect_tiles),
        out_shape=(
            jax.ShapeDtypeStruct((blocks, comps, cells), BF16),
            jax.ShapeDtypeStruct((blocks, lown, width), BF16),
        ),
        in_specs=[anywhere] * 9,
        out_specs=(anywhere,) * 2,
        scratch_shapes=scratch,
        compiler_params=pltpu.CompilerParams(
            collective_id=0, has_side_effects=True, vmem_limit_bytes=67043328
        ),
    )(
        spectrum, courant_x.reshape(1, comps), courant_y.reshape(1, comps),
        growth, quartet, coupler, atmosphere, ocean_state, sea_mask,
    )
    return pl.pallas_call(
        unpack_kernel,
        out_shape=(jax.ShapeDtypeStruct(spectrum.shape, BF16), column, column),
        in_specs=[anywhere] * 2,
        out_specs=(anywhere,) * 3,
        scratch_shapes=[
            v((blocks, comps, cells), BF16), v((blocks, lown, width), BF16), v(atmosphere.shape, F32), v(atmosphere.shape, F32),
            v((comps * rows, width), F32), v(spectrum.shape, BF16), dma((blocks + 1,)), dma((5,)),
        ],
        compiler_params=pltpu.CompilerParams(vmem_limit_bytes=67043328),
    )(*packed)


def fits_fused(mesh, spectrum, coupler, atmosphere):
    lev_parts = lax.axis_size("lev")
    cells = lax.axis_size("cells")
    blocks = cells * lev_parts
    comps, rows, width = spectrum.shape
    return (
        lev_parts == 2 and cells == 4 and lax.axis_size("sect") % 2 == 0 and width == LANES
        and comps % 16 == 0 and rows == 2 * blocks and (comps * blocks) % LANES == 0
        and atmosphere.shape[0] % 16 == 0 and 2 * atmosphere.shape[1] == blocks
    )


def solution(mesh):
    in_specs = (
        P(("cells", "lev"), "groups", "sect"),
        P(("cells", "lev")),
        P(("cells", "lev")),
        P(),
        P(),
        P(),
        P("lev", ("groups", "cells"), "sect"),
        P("lev", ("groups", "cells"), "sect"),
        P(("groups", "cells"), "sect"),
    )
    out_specs = (
        P(("cells", "lev"), "groups", "sect"),
        P("lev", ("groups", "cells"), "sect"),
        P("lev", ("groups", "cells"), "sect"),
    )

    def body(*args):
        if fits_fused(mesh, args[0], args[5], args[6]):
            return fused(*args)
        return on_device(*args)

    return jax.shard_map(
        body, mesh=mesh, in_specs=in_specs, out_specs=out_specs, check_vma=False
    )
```

profile of v0, /device:TPU:0, one launch (start us, length us, event | category | flops | bytes accessed | tf_op | source)
XLA Modules:
  0.0 49.3 jit_solution(17402699434544754105)
XLA Ops:
  0.6 44.5 %shard_map.112 = (bf16[8,144,256]{2,1,0:T(8,128)(2,1)}, bf16[8,32,128]{2,1,0:T(8,128)(2,1)}) custom-call(bf16[144,16,128]{2,1,0:T(8,128)(2,1)} %spec_hbm.1, f32[1,144]{1,0:T(1,128)} %bitcast.2, f32[1,144]{1,0:T(1,128)} %bitcast.3, f32[1152]{0:T(1024)} %growth_hbm.1, bf16[1152,1152]{1,0:T(8,128)(2,1)} %quartet_hbm.1, bf16[128,1152]{1,0:T(8,128)(2,1)} %coupler_hbm.1, ...), custom_call_target="tpu_custom_call" | custom-call | tf_op jit(solution)/shard_map/pallas_call | solution.py:680
  45.1 4.2 %shard_map.113 = (bf16[144,16,128]{2,1,0:T(8,128)(2,1)}, f32[32,4,128]{2,1,0:T(4,128)}, f32[32,4,128]{2,1,0:T(4,128)}) custom-call(bf16[8,144,256]{2,1,0:T(8,128)(2,1)} %get-tuple-element.5.ret, bf16[8,32,128]{2,1,0:T(8,128)(2,1)} %get-tuple-element.6.fin), custom_call_target="tpu_custom_call" | custom-call | tf_op jit(solution)/shard_map/pallas_call | solution.py:696
where the time goes:
time: 49.5 us; the launch traced here: 49.3 us
  Pallas kernels  48.7 us (98%)
  between operations  0.64 us (1%)
    pallas_call x1, Pallas kernels, fused(): pl.pallas_call(functools.partial(fused_kernel, cell_tiles, lev_parts, sec...  44.5 us
    pallas_call x1, Pallas kernels, fused(): pl.pallas_call(unpack_kernel, out_shape=(jax.ShapeDtypeStruct(spectrum.sh...  4.21 us

commit v1 on v0

--- a/solution.py
+++ b/solution.py
@@ -307,7 +307,7 @@
         def _():
             cell_f[part(me), cut] = send_f[spot, h]
 
-    chunk = 16
+    chunk = comps
     small = lax.broadcasted_iota(jnp.int32, (chunk, width), 1)
     at_rim = inside < lev_parts
 
@@ -596,39 +596,29 @@
         store.wait()
 
 
-def unpack_kernel(ret, fin, spec_out, atm_out, oce_out, ret_v, fin_v, atm_v, oce_v, flat, spec_v, in_sem, out_sem):
-    blocks, comps, cells = ret_v.shape
+def unpack_kernel(ret, fin, spec_out, atm_out, oce_out, atm_v, oce_v, flat, spec_v, out_sem):
+    blocks, comps, cells = ret.shape
     rows, width = spec_v.shape[1:]
     lines = cells // width
     seg = width // blocks
     tile_rows = atm_v.shape[1]
-    loads = [pltpu.make_async_copy(ret.at[b], ret_v.at[b], in_sem.at[b]) for b in range(blocks)]
-    loads.append(pltpu.make_async_copy(fin, fin_v, in_sem.at[blocks]))
-    for load in loads:
-        load.start()
-    loads[-1].wait()
     stores = []
-    groups = swap_groups([fin_v[t].astype(F32) for t in range(blocks)], seg)
+    for h in range(lines):
+        groups = swap_groups([ret[t, :, h * width:(h + 1) * width].astype(F32) for t in range(blocks)], seg)
+        for g, line in enumerate(groups):
+            flat[pl.ds(h * blocks + g, comps, stride=rows), :] = line
+    pieces = 3 if comps % 3 == 0 else 1
+    size = comps // pieces
+    for p in range(pieces):
+        cut = pl.ds(p * size, size)
+        spec_v[cut] = flat[pl.ds(p * size * rows, size * rows), :].reshape(size, rows, width).astype(BF16)
+        stores.append(pltpu.make_async_copy(spec_v.at[cut], spec_out.at[cut], out_sem.at[2 + p]))
+        stores[-1].start()
+    groups = swap_groups([fin[t].astype(F32) for t in range(blocks)], seg)
     for f, (target, out) in enumerate(((atm_v, atm_out), (oce_v, oce_out))):
         for r in range(tile_rows):
             target[:, r, :] = groups[f * tile_rows + r]
         stores.append(pltpu.make_async_copy(target, out, out_sem.at[f]))
-        stores[-1].start()
-    for load in loads[:-1]:
-        load.wait()
-    pieces = 3 if comps % 48 == 0 else 1
-    size = comps // pieces
-    for p in range(pieces):
-        for k in range(p * size, (p + 1) * size, 16):
-            for h in range(lines):
-                groups = swap_groups([
-                    ret_v[t, k:k + 16, h * width:(h + 1) * width].astype(F32) for t in range(blocks)
-                ], seg)
-                for g, line in enumerate(groups):
-                    flat[pl.ds(k * rows + h * blocks + g, 16, stride=rows), :] = line
-            spec_v[k:k + 16] = flat[k * rows:(k + 16) * rows, :].reshape(16, rows, width).astype(BF16)
-        cut = pl.ds(p * size, size)
-        stores.append(pltpu.make_async_copy(spec_v.at[cut], spec_out.at[cut], out_sem.at[2 + p]))
         stores[-1].start()
     for store in stores:
         store.wait()
@@ -676,33 +666,32 @@
         dma((blocks,)), dma((blocks,)),
     ]
     anywhere = pl.BlockSpec(memory_space=pltpu.HBM)
+    here = pl.BlockSpec(memory_space=pltpu.VMEM)
     column = jax.ShapeDtypeStruct(atmosphere.shape, F32)
     packed = pl.pallas_call(
         functools.partial(fused_kernel, cell_tiles, lev_parts, sect_tiles),
-        out_shape=(
-            jax.ShapeDtypeStruct((blocks, comps, cells), BF16),
-            jax.ShapeDtypeStruct((blocks, lown, width), BF16),
-        ),
+        out_shape=(v((blocks, comps, cells), BF16), v((blocks, lown, width), BF16)),
         in_specs=[anywhere] * 9,
-        out_specs=(anywhere,) * 2,
+        out_specs=(here,) * 2,
         scratch_shapes=scratch,
         compiler_params=pltpu.CompilerParams(
-            collective_id=0, has_side_effects=True, vmem_limit_bytes=67043328
+            collective_id=0, has_side_effects=True, vmem_limit_bytes=33554432
         ),
-    )(
-        spectrum, courant_x.reshape(1, comps), courant_y.reshape(1, comps),
-        growth, quartet, coupler, atmosphere, ocean_state, sea_mask,
-    )
+    )(*(
+        pltpu.with_memory_space_constraint(x, pltpu.HBM)
+        for x in (spectrum, courant_x.reshape(1, comps), courant_y.reshape(1, comps),
+                  growth, quartet, coupler, atmosphere, ocean_state, sea_mask)
+    ))
     return pl.pallas_call(
         unpack_kernel,
         out_shape=(jax.ShapeDtypeStruct(spectrum.shape, BF16), column, column),
-        in_specs=[anywhere] * 2,
+        in_specs=[here] * 2,
         out_specs=(anywhere,) * 3,
         scratch_shapes=[
-            v((blocks, comps, cells), BF16), v((blocks, lown, width), BF16), v(atmosphere.shape, F32), v(atmosphere.shape, F32),
-            v((comps * rows, width), F32), v(spectrum.shape, BF16), dma((blocks + 1,)), dma((5,)),
+            v(atmosphere.shape, F32), v(atmosphere.shape, F32),
+            v((comps * rows, width), F32), v(spectrum.shape, BF16), dma((5,)),
         ],
-        compiler_params=pltpu.CompilerParams(vmem_limit_bytes=67043328),
+        compiler_params=pltpu.CompilerParams(vmem_limit_bytes=33554432),
     )(*packed)
 
 

time: 49.5 us -> 46.6 us (0.941)
  Pallas kernels: 48.7 us -> 45.8 us
    pallas_call x1, Pallas kernels: 4.21 us -> 1.99 us  [fused(): pl.pallas_call(unpack_kernel, out_shape=(jax.ShapeDtypeStruct(spectrum.sh...]
    pallas_call x1, Pallas kernels: 44.5 us -> 43.8 us  [fused(): pl.pallas_call(functools.partial(fused_kernel, cell_tiles, lev_parts, sec...]
where the time goes in v1:
time: 46.6 us; the launch traced here: 46.4 us
  Pallas kernels  45.8 us (98%)
  between operations  0.64 us (1%)
    pallas_call x1, Pallas kernels, fused(): pl.pallas_call(functools.partial(fused_kernel, cell_tiles, lev_parts, sec...  43.8 us
    pallas_call x1, Pallas kernels, fused(): pl.pallas_call(unpack_kernel, out_shape=(jax.ShapeDtypeStruct(spectrum.sh...  1.99 us

profile of v1, /device:TPU:0, one launch (start us, length us, event | category | flops | bytes accessed | tf_op | source)
XLA Modules:
  0.0 46.4 jit_solution(11690229277561427819)
XLA Ops:
  0.6 43.8 %shard_map.112 = (bf16[8,144,256]{2,1,0:T(8,128)(2,1)S(1)}, bf16[8,32,128]{2,1,0:T(8,128)(2,1)S(1)}) custom-call(bf16[144,16,128]{2,1,0:T(8,128)(2,1)} %spec_hbm.1, f32[1,144]{1,0:T(1,128)} %bitcast.2, f32[1,144]{1,0:T(1,128)} %bitcast.3, f32[1152]{0:T(1024)} %growth_hbm.1, bf16[1152,1152]{1,0:T(8,128)(2,1)} %quartet_hbm.1, bf16[128,1152]{1,0:T(8,128)(2,1)} %coupler_hbm.1, ...), custom_call_target="tpu_custom_call" | custom-call | tf_op jit(solution)/shard_map/pallas_call | solution.py:671
  44.4 2.0 %shard_map.113 = (bf16[144,16,128]{2,1,0:T(8,128)(2,1)}, f32[32,4,128]{2,1,0:T(4,128)}, f32[32,4,128]{2,1,0:T(4,128)}) custom-call(bf16[8,144,256]{2,1,0:T(8,128)(2,1)S(1)} %get-tuple-element.5.ret, bf16[8,32,128]{2,1,0:T(8,128)(2,1)S(1)} %get-tuple-element.6.fin), custom_call_target="tpu_custom_call" | custom-call | tf_op jit(solution)/shard_map/pallas_call | solution.py:685

commit v2 on v1

--- a/solution.py
+++ b/solution.py
@@ -223,6 +223,28 @@
         pl.semaphore_signal(barrier, inc=1, device_id=side_id,
                             device_id_type=pl.DeviceIdType.MESH)
 
+    my_levels = pl.ds(pl.multiple_of(mine_l * lown, 16), lown)
+
+    def state_in(b):
+        return remote(swap_send.at[tile_of(b)], st_in.at[mine_c, my_levels, :], swap_ss.at[b],
+                      swap_rs.at[mine_c, mine_l], block_id(b))
+
+    def sea_over(c):
+        return remote(sea_send.at[tile_of(c * lev_parts + mine_l)], sea_in.at[mine_c], sea_ss.at[c],
+                      sea_rs.at[mine_c], {"cells": c})
+
+    loads[3].wait()
+    loads[4].wait()
+    loads[5].wait()
+    groups = [col_in[f, :, r, :] for f in range(2) for r in range(tile_rows)]
+    for t, line in enumerate(swap_groups(groups, seg)):
+        swap_send[t] = line.astype(BF16)
+    groups = [jnp.broadcast_to(sea_v[r:r + 1, :].astype(F32), (8, width)) for r in range(tile_rows)]
+    for t, line in enumerate(swap_groups(groups + [jnp.zeros((8, width), F32)] * tile_rows, seg)):
+        sea_send[t] = line[0:1]
+    st_in[mine_c, my_levels, :] = swap_send[spot]
+    sea_in[mine_c] = sea_send[spot]
+
     lane = lax.broadcasted_iota(jnp.int32, (comps, width), 1)
     loads[0].wait()
     flat[...] = spec_v[...].astype(F32).reshape(comps * rows, width)
@@ -252,7 +274,14 @@
         return copies
 
     edges = send_edges(0)
-
+    wave = [mirrored(i) for i in sorted(range(blocks), key=lambda i: (abs(2 * i + 1 - blocks), -i))]
+
+    for b in wave:
+        @pl.when(b != me)
+        def _():
+            state_in(b).start()
+    for dc in range(1, cell_tiles):
+        sea_over(lax.rem(mine_c + dc, cell_tiles)).start()
     loads[1].wait()
     loads[2].wait()
     for d, b in enumerate(order):
@@ -261,33 +290,6 @@
             copy.start()
             pending.append(copy)
 
-    my_levels = pl.ds(pl.multiple_of(mine_l * lown, 16), lown)
-
-    def state_in(b):
-        return remote(swap_send.at[tile_of(b)], st_in.at[mine_c, my_levels, :], swap_ss.at[b],
-                      swap_rs.at[mine_c, mine_l], block_id(b))
-
-    def sea_over(c):
-        return remote(sea_send.at[tile_of(c * lev_parts + mine_l)], sea_in.at[mine_c], sea_ss.at[c],
-                      sea_rs.at[mine_c], {"cells": c})
-
-    def send_state_in():
-        loads[3].wait()
-        loads[4].wait()
-        loads[5].wait()
-        groups = [col_in[f, :, r, :] for f in range(2) for r in range(tile_rows)]
-        for t, line in enumerate(swap_groups(groups, seg)):
-            swap_send[t] = line.astype(BF16)
-        groups = [jnp.broadcast_to(sea_v[r:r + 1, :].astype(F32), (8, width)) for r in range(tile_rows)]
-        for t, line in enumerate(swap_groups(groups + [jnp.zeros((8, width), F32)] * tile_rows, seg)):
-            sea_send[t] = line[0:1]
-        for b in order:
-            state_in(b).start()
-        for dc in range(1, cell_tiles):
-            sea_over(lax.rem(mine_c + dc, cell_tiles)).start()
-        st_in[mine_c, my_levels, :] = swap_send[spot]
-        sea_in[mine_c] = sea_send[spot]
-
     def halves(c):
         return jnp.maximum(c, 0.0), jnp.maximum(-c, 0.0)
 
@@ -309,7 +311,6 @@
 
     chunk = comps
     small = lax.broadcasted_iota(jnp.int32, (chunk, width), 1)
-    at_rim = inside < lev_parts
 
     for h in range(lines):
         for k in range(0, comps, chunk):
@@ -334,15 +335,18 @@
                     send_f[t, h, k:k + chunk] = line.astype(BF16)
                 else:
                     outer[min(t, 1), h, k:k + chunk] = line
-        for i in range(blocks - 2, half - 1, -1):
-            send_line(mirrored(i), h)
-        send_line(mirrored(1), h)
-
-        @pl.when(jnp.logical_not(at_rim))
-        def _():
-            for i in range(2, half):
-                send_line(mirrored(i), h)
-    send_state_in()
+        for b in wave[:2]:
+            send_line(b, h)
+    for b in wave[2:4]:
+        for h in range(lines):
+            send_line(b, h)
+
+    @pl.when(inside != half - 1)
+    def _():
+        for h in range(lines):
+            send_line(wave[4], h)
+    for h in range(lines):
+        send_line(wave[5], h)
     for copy in edges:
         copy.wait_recv()
     for k in range(0, comps, chunk):
@@ -355,15 +359,13 @@
             east_part = jnp.where(small % seg == seg - 1, pltpu.roll(from_east, seg - 1 - h, 1), 0.0)
             send_f[0, h, k:k + chunk] = (outer[0, h, k:k + chunk] + px * west_part).astype(BF16)
             send_f[blocks - 1, h, k:k + chunk] = (outer[1, h, k:k + chunk] + mx * east_part).astype(BF16)
-    for i in (blocks - 1, 0):
+
+    @pl.when(inside != half - 1)
+    def _():
         for h in range(lines):
-            send_line(mirrored(i), h)
-
-    @pl.when(at_rim)
-    def _():
-        for i in range(2, half):
-            for h in range(lines):
-                send_line(mirrored(i), h)
+            send_line(wave[6], h)
+    for h in range(lines):
+        send_line(wave[7], h)
 
     level_id = lax.broadcasted_iota(jnp.int32, (levels, width), 0)
     level_lane = lax.broadcasted_iota(jnp.int32, (levels, width), 1)
@@ -503,6 +505,12 @@
     edge_send[1, 0] = first.astype(BF16)
     edge_send[1, 1] = last.astype(BF16)
     edges = send_edges(1)
+
+    @pl.when(inside == half - 1)
+    def _():
+        for i in (4, 6):
+            for h in range(lines):
+                send_line(wave[i], h)
 
     west_rim = lane % seg == 0
     east_rim = lane % seg == seg - 1

time: 46.6 us -> 43.7 us (0.938)
  Pallas kernels: 45.8 us -> 42.9 us
    pallas_call x1, Pallas kernels: 43.8 us -> 40.9 us  [fused(): pl.pallas_call(functools.partial(fused_kernel, cell_tiles, lev_parts, sec...]
where the time goes in v2:
time: 43.7 us; the launch traced here: 43.5 us
  Pallas kernels  42.9 us (98%)
  between operations  0.64 us (1%)
    pallas_call x1, Pallas kernels, fused(): pl.pallas_call(functools.partial(fused_kernel, cell_tiles, lev_parts, sec...  40.9 us
    pallas_call x1, Pallas kernels, fused(): pl.pallas_call(unpack_kernel, out_shape=(jax.ShapeDtypeStruct(spectrum.sh...  1.99 us

profile of v2, /device:TPU:0, one launch (start us, length us, event | category | flops | bytes accessed | tf_op | source)
XLA Modules:
  0.0 43.5 jit_solution(6320514314464113122)
XLA Ops:
  0.6 40.9 %shard_map.112 = (bf16[8,144,256]{2,1,0:T(8,128)(2,1)S(1)}, bf16[8,32,128]{2,1,0:T(8,128)(2,1)S(1)}) custom-call(bf16[144,16,128]{2,1,0:T(8,128)(2,1)} %spec_hbm.1, f32[1,144]{1,0:T(1,128)} %bitcast.2, f32[1,144]{1,0:T(1,128)} %bitcast.3, f32[1152]{0:T(1024)} %growth_hbm.1, bf16[1152,1152]{1,0:T(8,128)(2,1)} %quartet_hbm.1, bf16[128,1152]{1,0:T(8,128)(2,1)} %coupler_hbm.1, ...), custom_call_target="tpu_custom_call" | custom-call | tf_op jit(solution)/shard_map/pallas_call | solution.py:679
  41.5 2.0 %shard_map.113 = (bf16[144,16,128]{2,1,0:T(8,128)(2,1)}, f32[32,4,128]{2,1,0:T(4,128)}, f32[32,4,128]{2,1,0:T(4,128)}) custom-call(bf16[8,144,256]{2,1,0:T(8,128)(2,1)S(1)} %get-tuple-element.5.ret, bf16[8,32,128]{2,1,0:T(8,128)(2,1)S(1)} %get-tuple-element.6.fin), custom_call_target="tpu_custom_call" | custom-call | tf_op jit(solution)/shard_map/pallas_call | solution.py:693

commit v3 on v2

--- a/solution.py
+++ b/solution.py
@@ -9,6 +9,7 @@
 
 NSTEP = 2
 LANES = 128
+HELD = {6: {3: "edges", 2: "far"}}
 F32 = jnp.float32
 BF16 = jnp.bfloat16
 
@@ -144,10 +145,10 @@
     cell_tiles, lev_parts, sect_tiles,
     spec_hbm, cx_hbm, cy_hbm, growth_hbm, quartet_hbm, coupler_hbm, atm_hbm, oce_hbm, sea_hbm,
     ret, fin,
-    spec_v, cx_v, cy_v, growth_v, quartet_v, coupler_v, col_in, sea_v,
-    flat, rows_v, send_f, cell_f, cell_s, cx_all, cy_all, cxb, cyb, grow_b,
+    spec_v, c_v, growth_v, quartet_v, coupler_v, col_in, sea_v,
+    flat, rows_v, send_f, cell_f, cell_s, c_all, cxb, cyb, grow_b,
     edge_send, edge_recv, e1, e2,
-    swap_send, st_in, sea_send, sea_in, outer, inner, st0, st1, st2, st_edge_send, st_edge_recv, st_back,
+    swap_send, st_in, sea_send, sea_in, outer, inner, stage_v, total_v, st0, st1, st2, st_edge_send, st_edge_recv, st_back,
     in_sem, own_sem, f_send, f_recv, c_send, c_recv,
     edge_ss, edge_rs, swap_ss, swap_rs, sea_ss, sea_rs, back_ss, back_rs, ste_ss, ste_rs,
     ret_ss, ret_rs,
@@ -158,6 +159,7 @@
     lown = col_in.shape[1]
     tile_rows = col_in.shape[2]
     levels = lown * lev_parts
+    cells = lines * width
     seg = width // blocks
     mid = width // 2
     mine_c = lax.axis_index("cells")
@@ -207,11 +209,14 @@
     loads = [
         pltpu.make_async_copy(a, b, in_sem.at[i])
         for i, (a, b) in enumerate([
-            (spec_hbm, spec_v), (cx_hbm, cx_v), (cy_hbm, cy_v),
+            (spec_hbm, spec_v), (cx_hbm, c_v.at[0]), (cy_hbm, c_v.at[1]),
             (atm_hbm, col_in.at[0]), (oce_hbm, col_in.at[1]), (sea_hbm, sea_v),
             (growth_hbm, growth_v), (coupler_hbm, coupler_v), (quartet_hbm, quartet_v),
         ])
     ]
+
+    def whole(ref, sem):
+        return remote(ref, ref, sem, sem, {"lev": 1 - mine_l})
     for load in loads:
         load.start()
 
@@ -226,12 +231,12 @@
     my_levels = pl.ds(pl.multiple_of(mine_l * lown, 16), lown)
 
     def state_in(b):
-        return remote(swap_send.at[tile_of(b)], st_in.at[mine_c, my_levels, :], swap_ss.at[b],
-                      swap_rs.at[mine_c, mine_l], block_id(b))
+        return remote(swap_send.at[tile_of(b)], st_in.at[mine_c, my_levels, :], swap_ss.at[0],
+                      swap_rs.at[0], block_id(b))
 
     def sea_over(c):
-        return remote(sea_send.at[tile_of(c * lev_parts + mine_l)], sea_in.at[mine_c], sea_ss.at[c],
-                      sea_rs.at[mine_c], {"cells": c})
+        return remote(sea_send.at[tile_of(c * lev_parts + mine_l)], sea_in.at[mine_c], sea_ss.at[0],
+                      sea_rs.at[0], {"cells": c})
 
     loads[3].wait()
     loads[4].wait()
@@ -260,20 +265,15 @@
     edge_send[0, 1] = last.astype(BF16)
 
     pl.semaphore_wait(barrier, blocks + 3)
-    pending = []
-
     def send_edges(step):
         copies = [
-            remote(edge_send.at[step, i], edge_recv.at[step, i],
-                   edge_ss.at[step, i], edge_rs.at[step, i], where)
+            remote(edge_send.at[step, i], edge_recv.at[step, i], edge_ss.at[0], edge_rs.at[step], where)
             for i, where in enumerate((west, east) if step == 0 else (near_west, near_east))
         ]
         for copy in copies:
             copy.start()
-        pending.extend(copies)
-        return copies
-
-    edges = send_edges(0)
+
+    send_edges(0)
     wave = [mirrored(i) for i in sorted(range(blocks), key=lambda i: (abs(2 * i + 1 - blocks), -i))]
 
     for b in wave:
@@ -284,17 +284,14 @@
         sea_over(lax.rem(mine_c + dc, cell_tiles)).start()
     loads[1].wait()
     loads[2].wait()
-    for d, b in enumerate(order):
-        for i, (src, dst) in enumerate(((cx_v, cx_all), (cy_v, cy_all))):
-            copy = remote(src, dst.at[me], c_send.at[i, d], c_recv.at[i, me], block_id(b))
-            copy.start()
-            pending.append(copy)
+    for b in order:
+        remote(c_v, c_all.at[me], c_send.at[0], c_recv.at[0], block_id(b)).start()
 
     def halves(c):
         return jnp.maximum(c, 0.0), jnp.maximum(-c, 0.0)
 
-    cxb[part(me), :] = jnp.broadcast_to(column_of(cx_v[...]), (comps, width))
-    cyb[part(me), :] = jnp.broadcast_to(column_of(cy_v[...]), (comps, width))
+    cxb[part(me), :] = jnp.broadcast_to(column_of(c_v[0]), (comps, width))
+    cyb[part(me), :] = jnp.broadcast_to(column_of(c_v[1]), (comps, width))
 
     def send_line(b, h):
         t = tile_of(b)
@@ -302,7 +299,7 @@
 
         @pl.when(b != me)
         def _():
-            remote(send_f.at[t, h], cell_f.at[part(me), cut], f_send.at[b, h], f_recv.at[me, h],
+            remote(send_f.at[t, h], cell_f.at[part(me), cut], f_send.at[0], f_recv.at[me],
                    block_id(b)).start()
 
         @pl.when(b == me)
@@ -312,6 +309,7 @@
     chunk = comps
     small = lax.broadcasted_iota(jnp.int32, (chunk, width), 1)
 
+    early = [jnp.where(inside < lev_parts, wave[i], wave[j]) for i, j in ((1, 0), (3, 1), (0, 2), (2, 3))]
     for h in range(lines):
         for k in range(0, comps, chunk):
             own = pl.ds(pl.multiple_of(me * comps + k, 16), chunk)
@@ -335,20 +333,34 @@
                     send_f[t, h, k:k + chunk] = line.astype(BF16)
                 else:
                     outer[min(t, 1), h, k:k + chunk] = line
-        for b in wave[:2]:
+        for b in early[:2]:
             send_line(b, h)
-    for b in wave[2:4]:
+    for b in early[2:]:
         for h in range(lines):
             send_line(b, h)
 
-    @pl.when(inside != half - 1)
-    def _():
-        for h in range(lines):
-            send_line(wave[4], h)
+    def release(now, position):
+        ready = [p for p, when in HELD.get(position, {}).items() if when == now]
+        if now == "start":
+            late = [p for p, when in HELD.get(position, {}).items() if when != now]
+            ready = [p for p in range(half) if p not in late]
+        if len(ready) == half:
+            for h in range(lines):
+                send_line(wave[position], h)
+        elif ready:
+            hit = inside == ready[0]
+            for p in ready[1:]:
+                hit = hit | (inside == p)
+
+            @pl.when(hit)
+            def _():
+                for h in range(lines):
+                    send_line(wave[position], h)
+
+    release("start", 4)
     for h in range(lines):
         send_line(wave[5], h)
-    for copy in edges:
-        copy.wait_recv()
+    whole(edge_recv.at[0], edge_rs.at[0]).wait_recv()
     for k in range(0, comps, chunk):
         cx = cxb[pl.ds(pl.multiple_of(me * comps + k, 16), chunk), :]
         px, mx = halves(cx)
@@ -359,11 +371,7 @@
             east_part = jnp.where(small % seg == seg - 1, pltpu.roll(from_east, seg - 1 - h, 1), 0.0)
             send_f[0, h, k:k + chunk] = (outer[0, h, k:k + chunk] + px * west_part).astype(BF16)
             send_f[blocks - 1, h, k:k + chunk] = (outer[1, h, k:k + chunk] + mx * east_part).astype(BF16)
-
-    @pl.when(inside != half - 1)
-    def _():
-        for h in range(lines):
-            send_line(wave[6], h)
+    release("start", 6)
     for h in range(lines):
         send_line(wave[7], h)
 
@@ -389,14 +397,8 @@
             east_pack = jnp.where(fold_place == slot, pltpu.roll(v, (slot + 1 - seg) % width, 1), east_pack)
         st_edge_send[step, 0] = west_pack
         st_edge_send[step, 1] = east_pack
-        copies = []
         for i, where in enumerate((near_west, near_east)):
-            copies.append(remote(st_edge_send.at[step, i], st_edge_recv.at[step, i],
-                                 ste_ss.at[step, i], ste_rs.at[step, i], where))
-        for copy in copies:
-            copy.start()
-        pending.extend(copies)
-        return copies
+            remote(st_edge_send.at[step, i], st_edge_recv.at[step, i], ste_ss.at[0], ste_rs.at[step], where).start()
 
     def update(state, new, step, profile):
         rim_west = (mine_x == 0) & (spot == 0)
@@ -438,10 +440,7 @@
             out.append(diff * diff)
         return out
 
-    def fresh_part(b, wind_rows, target):
-        weights = quartet_v[part(b), :]
-        pair = jnp.dot(weights, cell_f[...], preferred_element_type=F32)
-        quad = jnp.dot(weights, cell_s[...], preferred_element_type=F32)
+    def fresh_part(b, wind_rows, target, pair, quad):
         outs = []
         for r in range(lines):
             cut = slice(r * width, (r + 1) * width)
@@ -452,24 +451,13 @@
             outs.append(out)
         return outs
 
-    def square(b):
-        f = cell_f[part(b), :].astype(F32)
-        cell_s[part(b), :] = (f * f).astype(BF16)
-
-    square(me)
-    for b in order[::-1]:
-        for i, dst in enumerate((cx_all, cy_all)):
-            remote(dst.at[b], dst.at[b], c_send.at[i, 0], c_recv.at[i, b], block_id(b)).wait_recv()
-        cxb[part(b), :] = jnp.broadcast_to(column_of(cx_all[b]), (comps, width))
-        cyb[part(b), :] = jnp.broadcast_to(column_of(cy_all[b]), (comps, width))
-    for b in order[::-1]:
-        c = lax.div(b, lev_parts)
-        core = lax.rem(b, lev_parts)
-        there = st_in.at[c, pl.ds(pl.multiple_of(core * lown, 16), lown), :]
-        remote(there, there, swap_ss.at[0], swap_rs.at[c, core], block_id(b)).wait_recv()
-    for dc in range(1, cell_tiles):
-        c = lax.rem(mine_c + dc, cell_tiles)
-        remote(sea_in.at[c], sea_in.at[c], sea_ss.at[0], sea_rs.at[c], {"cells": c}).wait_recv()
+    others = pl.ds(0, blocks - 1)
+    whole(c_all.at[others], c_recv.at[0]).wait_recv()
+    for b in order:
+        cxb[part(b), :] = jnp.broadcast_to(column_of(c_all[b, 0]), (comps, width))
+        cyb[part(b), :] = jnp.broadcast_to(column_of(c_all[b, 1]), (comps, width))
+    whole(swap_send.at[others], swap_rs.at[0]).wait_recv()
+    whole(sea_send.at[pl.ds(0, cell_tiles - 1)], sea_rs.at[0]).wait_recv()
 
     wide_lane = lax.broadcasted_iota(jnp.int32, (8, width), 1)
     sea = []
@@ -481,22 +469,51 @@
         low = jnp.broadcast_to(sea_in[2 * h], (8, width))
         high = jnp.broadcast_to(sea_in[2 * h + 1], (8, width))
         sea.append(jnp.where(wide_lane < mid, low, pltpu.roll(high, mid, 1))[0:1])
-    state_copies = send_state(st0, 0)
+    send_state(st0, 0)
 
     loads[7].wait()
     loads[8].wait()
-    for b in order[::-1]:
-        for h in range(lines):
-            cut = slice(h * width, (h + 1) * width)
-            remote(cell_f.at[part(b), cut], cell_f.at[part(b), cut], f_send.at[0, 0], f_recv.at[b, h],
-                   block_id(b)).wait_recv()
-        square(b)
+
+    near = half * comps
+    span = stage_v.shape[2]
+    spare = span - near
+    for i in range(2):
+        for x in range(2):
+            stage_v[i, x, (1 - i) * near:(1 - i) * near + spare] = jnp.zeros((spare, cells), BF16)
+
+    def stage(b):
+        f = cell_f[part(b), :]
+        wide = f.astype(F32)
+        which = lax.div(b, half)
+        rows_of = pl.ds(pl.multiple_of(which * spare + (b - which * half) * comps, 16), comps)
+        stage_v[which, 0, rows_of, :] = f
+        stage_v[which, 1, rows_of, :] = (wide * wide).astype(BF16)
+
+    def products(rows_of, which):
+        weights = quartet_v[rows_of, pl.ds(pl.multiple_of(which * (quartet_v.shape[1] - span), LANES), span)]
+        return [jnp.dot(weights, stage_v[which, i], preferred_element_type=F32) for i in range(2)]
+
+    def arrived(b):
+        whole(cell_f.at[part(b), :], f_recv.at[b]).wait_recv()
+        stage(b)
+
+    stage(me)
+    for b in order[half:][::-1]:
+        arrived(b)
+    for m in range(blocks):
+        for i, x in enumerate(products(part(m), side)):
+            total_v[i, part(m), :] = x
+    for b in order[:half][::-1]:
+        arrived(b)
+    release("far", 6)
 
     wind_rows = wind(st0)
     first = jnp.zeros((comps, width), F32)
     last = jnp.zeros((comps, width), F32)
     for b in range(blocks):
-        outs = fresh_part(b, wind_rows, e1)
+        pair, quad = [total_v[i, part(b), :] + x
+                      for i, x in enumerate(products(part(b), 1 - side))]
+        outs = fresh_part(b, wind_rows, e1, pair, quad)
         for r in range(lines):
             slot = b * lines + r
             v = outs[r].astype(F32)
@@ -504,13 +521,8 @@
             last = jnp.where(lane % seg == slot, pltpu.roll(v, (slot + 1 - seg) % width, 1), last)
     edge_send[1, 0] = first.astype(BF16)
     edge_send[1, 1] = last.astype(BF16)
-    edges = send_edges(1)
-
-    @pl.when(inside == half - 1)
-    def _():
-        for i in (4, 6):
-            for h in range(lines):
-                send_line(wave[i], h)
+    send_edges(1)
+    release("edges", 6)
 
     west_rim = lane % seg == 0
     east_rim = lane % seg == seg - 1
@@ -531,14 +543,12 @@
                 v * keep + px * to_west + mx * to_east + py * north + my * south
             )
 
-    for copy in state_copies:
-        copy.wait_recv()
+    whole(st_edge_recv.at[0], ste_rs.at[0]).wait_recv()
     update(st0, st1, 0, jnp.dot(coupler_v[...], e1[...], preferred_element_type=F32))
-    state_copies = send_state(st1, 1)
+    send_state(st1, 1)
     wind_rows = wind(st1)
 
-    for copy in edges:
-        copy.wait_recv()
+    whole(edge_recv.at[1], edge_rs.at[1]).wait_recv()
     from_east = edge_recv[1, 0].astype(F32)
     from_west = edge_recv[1, 1].astype(F32)
     for b in range(blocks):
@@ -555,15 +565,15 @@
             wide = out.astype(F32)
             cell_s[part(b), cut] = (wide * wide).astype(BF16)
 
-    for d, b in enumerate(order + [me]):
-        fresh_part(b, wind_rows, e2)
-        if d < blocks - 1:
-            copy = remote(e2.at[part(b), :], ret.at[spot], ret_ss.at[d], ret_rs.at[spot], block_id(b))
-            copy.start()
-            pending.append(copy)
-
-    for copy in state_copies:
-        copy.wait_recv()
+    for b in order + [me]:
+        weights = quartet_v[part(b), :]
+        pair = jnp.dot(weights, cell_f[...], preferred_element_type=F32)
+        quad = jnp.dot(weights, cell_s[...], preferred_element_type=F32)
+        fresh_part(b, wind_rows, e2, pair, quad)
+        if b is not me:
+            remote(e2.at[part(b), :], ret.at[spot], ret_ss.at[0], ret_rs.at[0], block_id(b)).start()
+
+    whole(st_edge_recv.at[1], ste_rs.at[1]).wait_recv()
     update(st1, st2, 1, jnp.dot(coupler_v[...], e2[...], preferred_element_type=F32))
     for h in range(lines):
         atm = st2[0, h]
@@ -571,35 +581,28 @@
         st_back[2 * h] = jnp.where(level_lane < mid, atm, pltpu.roll(oce, mid, 1)).astype(BF16)
         st_back[2 * h + 1] = jnp.where(level_lane < mid, pltpu.roll(atm, mid, 1), oce).astype(BF16)
 
-    for d, b in enumerate(order):
+    for b in order:
         c = lax.div(b, lev_parts)
         core = lax.rem(b, lev_parts)
-        copy = remote(st_back.at[c, pl.ds(pl.multiple_of(core * lown, 16), lown), :], fin.at[spot], back_ss.at[d],
-                      back_rs.at[spot], block_id(b))
-        copy.start()
-        pending.append(copy)
+        remote(st_back.at[c, pl.ds(pl.multiple_of(core * lown, 16), lown), :], fin.at[spot], back_ss.at[0],
+               back_rs.at[0], block_id(b)).start()
     stores = [
         pltpu.make_async_copy(st_back.at[mine_c, my_levels, :], fin.at[spot], own_sem.at[0]),
         pltpu.make_async_copy(e2.at[part(me), :], ret.at[spot], own_sem.at[1]),
     ]
     for store in stores:
         store.start()
-    for b in order[::-1]:
-        t = tile_of(b)
-        remote(e2.at[part(b), :], ret.at[t], ret_ss.at[0], ret_rs.at[t], block_id(b)).wait_recv()
-    for b in order[::-1]:
-        t = tile_of(b)
-        remote(fin.at[t], fin.at[t], back_ss.at[0], back_rs.at[t], block_id(b)).wait_recv()
-
-    for b in order:
-        state_in(b).wait_send()
-        for h in range(lines):
-            remote(send_f.at[tile_of(b), h], send_f.at[tile_of(b), h], f_send.at[b, h], f_recv.at[0, 0],
-                   block_id(b)).wait_send()
-    for dc in range(1, cell_tiles):
-        sea_over(lax.rem(mine_c + dc, cell_tiles)).wait_send()
-    for copy in pending:
-        copy.wait_send()
+    whole(ret.at[others], ret_rs.at[0]).wait_recv()
+    whole(fin.at[others], back_rs.at[0]).wait_recv()
+
+    whole(send_f.at[others], f_send.at[0]).wait_send()
+    whole(c_all.at[others], c_send.at[0]).wait_send()
+    whole(swap_send.at[others], swap_ss.at[0]).wait_send()
+    whole(sea_send.at[pl.ds(0, cell_tiles - 1)], sea_ss.at[0]).wait_send()
+    whole(edge_send, edge_ss.at[0]).wait_send()
+    whole(st_edge_send, ste_ss.at[0]).wait_send()
+    whole(ret.at[others], ret_ss.at[0]).wait_send()
+    whole(fin.at[others], back_ss.at[0]).wait_send()
     for store in stores:
         store.wait()
 
@@ -649,29 +652,29 @@
     v = pltpu.VMEM
     dma = pltpu.SemaphoreType.DMA
     scratch = [
-        v((comps, rows, width), BF16), v((1, comps), F32), v((1, comps), F32),
+        v((comps, rows, width), BF16), v((2, 1, comps), F32),
         v((total,), F32), v((total, total), BF16), v(coupler.shape, BF16),
         v((2, lown, tile_rows, width), F32), v(sea_mask.shape, jnp.int32),
         v((comps * rows, width), F32), v((rows, comps, width), F32),
         v((blocks, lines, comps, width), BF16), v((total, cells), BF16), v((total, cells), BF16),
-        v((blocks, 1, comps), F32), v((blocks, 1, comps), F32),
+        v((blocks, 2, 1, comps), F32),
         v((total, width), F32), v((total, width), F32), v((total, width), F32),
         v((NSTEP, 2, comps, width), BF16), v((NSTEP, 2, comps, width), BF16),
         v((total, cells), BF16), v((total, cells), BF16),
         v((blocks, lown, width), BF16), v((cell_tiles, levels, width), BF16),
         v((blocks, 1, width), F32), v((cell_tiles, 1, width), F32),
         v((2, lines, comps, width), F32), v((total, cells), F32),
+        v((2, 2, -(-total // (2 * LANES)) * LANES, cells), BF16), v((2, total, cells), F32),
         v((2, lines, levels, width), F32), v((2, lines, levels, width), F32),
         v((2, lines, levels, width), F32),
         v((NSTEP, 2, depth, width), F32), v((NSTEP, 2, depth, width), F32),
         v((cell_tiles, levels, width), BF16),
-        dma((9,)), dma((2,)), dma((blocks, lines)), dma((blocks, lines)),
-        dma((2, blocks)), dma((2, blocks)),
-        dma((NSTEP, 2)), dma((NSTEP, 2)),
-        dma((blocks,)), dma((cell_tiles, lev_parts)), dma((cell_tiles,)), dma((cell_tiles,)),
-        dma((blocks,)), dma((blocks,)),
-        dma((NSTEP, 2)), dma((NSTEP, 2)),
-        dma((blocks,)), dma((blocks,)),
+        dma((9,)), dma((2,)), dma((1,)), dma((blocks,)), dma((1,)), dma((1,)),
+        dma((1,)), dma((NSTEP,)),
+        dma((1,)), dma((1,)), dma((1,)), dma((1,)),
+        dma((1,)), dma((1,)),
+        dma((1,)), dma((NSTEP,)),
+        dma((1,)), dma((1,)),
     ]
     anywhere = pl.BlockSpec(memory_space=pltpu.HBM)
     here = pl.BlockSpec(memory_space=pltpu.VMEM)

time: 43.7 us -> 41.8 us (0.957)
  Pallas kernels: 42.9 us -> 41 us
    pallas_call x1, Pallas kernels: 40.9 us -> 39 us  [fused(): pl.pallas_call(functools.partial(fused_kernel, cell_tiles, lev_parts, sec...]
where the time goes in v3:
time: 41.8 us; the launch traced here: 41.6 us
  Pallas kernels  41 us (98%)
  between operations  0.64 us (2%)
    pallas_call x1, Pallas kernels, fused(): pl.pallas_call(functools.partial(fused_kernel, cell_tiles, lev_parts, sec...  39 us
    pallas_call x1, Pallas kernels, fused(): pl.pallas_call(unpack_kernel, out_shape=(jax.ShapeDtypeStruct(spectrum.sh...  1.99 us

profile of v3, /device:TPU:0, one launch (start us, length us, event | category | flops | bytes accessed | tf_op | source)
XLA Modules:
  0.0 41.6 jit_solution(235890860355752188)
XLA Ops:
  0.6 39.0 %shard_map.112 = (bf16[8,144,256]{2,1,0:T(8,128)(2,1)S(1)}, bf16[8,32,128]{2,1,0:T(8,128)(2,1)S(1)}) custom-call(bf16[144,16,128]{2,1,0:T(8,128)(2,1)} %spec_hbm.1, f32[1,144]{1,0:T(1,128)} %bitcast.2, f32[1,144]{1,0:T(1,128)} %bitcast.3, f32[1152]{0:T(1024)} %growth_hbm.1, bf16[1152,1152]{1,0:T(8,128)(2,1)} %quartet_hbm.1, bf16[128,1152]{1,0:T(8,128)(2,1)} %coupler_hbm.1, ...), custom_call_target="tpu_custom_call" | custom-call | tf_op jit(solution)/shard_map/pallas_call | solution.py:682
  39.6 2.0 %shard_map.113 = (bf16[144,16,128]{2,1,0:T(8,128)(2,1)}, f32[32,4,128]{2,1,0:T(4,128)}, f32[32,4,128]{2,1,0:T(4,128)}) custom-call(bf16[8,144,256]{2,1,0:T(8,128)(2,1)S(1)} %get-tuple-element.5.ret, bf16[8,32,128]{2,1,0:T(8,128)(2,1)S(1)} %get-tuple-element.6.fin), custom_call_target="tpu_custom_call" | custom-call | tf_op jit(solution)/shard_map/pallas_call | solution.py:696

commit v4 on v3

--- a/solution.py
+++ b/solution.py
@@ -144,13 +144,13 @@
 def fused_kernel(
     cell_tiles, lev_parts, sect_tiles,
     spec_hbm, cx_hbm, cy_hbm, growth_hbm, quartet_hbm, coupler_hbm, atm_hbm, oce_hbm, sea_hbm,
-    ret, fin,
+    ret, fin, early,
     spec_v, c_v, growth_v, quartet_v, coupler_v, col_in, sea_v,
     flat, rows_v, send_f, cell_f, cell_s, c_all, cxb, cyb, grow_b,
-    edge_send, edge_recv, e1, e2,
+    side_send, side_recv, edge_send, edge_recv, e1, e2,
     swap_send, st_in, sea_send, sea_in, outer, inner, stage_v, total_v, st0, st1, st2, st_edge_send, st_edge_recv, st_back,
-    in_sem, own_sem, f_send, f_recv, c_send, c_recv,
-    edge_ss, edge_rs, swap_ss, swap_rs, sea_ss, sea_rs, back_ss, back_rs, ste_ss, ste_rs,
+    in_sem, f_send, f_recv, c_send, c_recv,
+    side_ss, side_rs, edge_ss, edge_rs, swap_ss, swap_rs, sea_ss, sea_rs, back_ss, back_rs, ste_ss, ste_rs,
     ret_ss, ret_rs,
 ):
     blocks = cell_tiles * lev_parts
@@ -250,30 +250,7 @@
     st_in[mine_c, my_levels, :] = swap_send[spot]
     sea_in[mine_c] = sea_send[spot]
 
-    lane = lax.broadcasted_iota(jnp.int32, (comps, width), 1)
-    loads[0].wait()
-    flat[...] = spec_v[...].astype(F32).reshape(comps * rows, width)
-    first = jnp.zeros((comps, width), F32)
-    last = jnp.zeros((comps, width), F32)
-    for r in range(rows):
-        v = flat[pl.ds(r, comps, stride=rows), :]
-        rows_v[r] = v
-        place = (r % blocks) * seg + r // blocks
-        first = jnp.where(lane == place, pltpu.roll(v, place, 1), first)
-        last = jnp.where(lane == place, pltpu.roll(v, (place + 1) % width, 1), last)
-    edge_send[0, 0] = first.astype(BF16)
-    edge_send[0, 1] = last.astype(BF16)
-
     pl.semaphore_wait(barrier, blocks + 3)
-    def send_edges(step):
-        copies = [
-            remote(edge_send.at[step, i], edge_recv.at[step, i], edge_ss.at[0], edge_rs.at[step], where)
-            for i, where in enumerate((west, east) if step == 0 else (near_west, near_east))
-        ]
-        for copy in copies:
-            copy.start()
-
-    send_edges(0)
     wave = [mirrored(i) for i in sorted(range(blocks), key=lambda i: (abs(2 * i + 1 - blocks), -i))]
 
     for b in wave:
@@ -287,6 +264,12 @@
     for b in order:
         remote(c_v, c_all.at[me], c_send.at[0], c_recv.at[0], block_id(b)).start()
 
+    lane = lax.broadcasted_iota(jnp.int32, (comps, width), 1)
+    loads[0].wait()
+    flat[...] = spec_v[...].astype(F32).reshape(comps * rows, width)
+    for r in range(rows):
+        rows_v[r] = flat[pl.ds(r, comps, stride=rows), :]
+
     def halves(c):
         return jnp.maximum(c, 0.0), jnp.maximum(-c, 0.0)
 
@@ -309,7 +292,7 @@
     chunk = comps
     small = lax.broadcasted_iota(jnp.int32, (chunk, width), 1)
 
-    early = [jnp.where(inside < lev_parts, wave[i], wave[j]) for i, j in ((1, 0), (3, 1), (0, 2), (2, 3))]
+    lead = [jnp.where(inside < lev_parts, wave[i], wave[j]) for i, j in ((1, 0), (3, 1), (0, 2), (2, 3))]
     for h in range(lines):
         for k in range(0, comps, chunk):
             own = pl.ds(pl.multiple_of(me * comps + k, 16), chunk)
@@ -333,9 +316,9 @@
                     send_f[t, h, k:k + chunk] = line.astype(BF16)
                 else:
                     outer[min(t, 1), h, k:k + chunk] = line
-        for b in early[:2]:
+        for b in lead[:2]:
             send_line(b, h)
-    for b in early[2:]:
+    for b in lead[2:]:
         for h in range(lines):
             send_line(b, h)
 
@@ -360,14 +343,25 @@
     release("start", 4)
     for h in range(lines):
         send_line(wave[5], h)
-    whole(edge_recv.at[0], edge_rs.at[0]).wait_recv()
+
+    edge = jnp.zeros((comps, width), F32)
+    for r in range(rows):
+        v = rows_v[r]
+        slot = (r % blocks) * seg + r // blocks
+        edge = jnp.where(lane == slot, pltpu.roll(v, slot, 1), edge)
+        edge = jnp.where(lane == slot + lines, pltpu.roll(v, (slot + lines + 1) % width, 1), edge)
+    side_send[...] = edge.astype(BF16)
+    sides = (west, east) if sect_tiles > 2 else (west,)
+    for i, where in enumerate(sides):
+        remote(side_send, side_recv.at[i], side_ss.at[0], side_rs.at[0], where).start()
+    whole(side_recv.at[pl.ds(0, len(sides))], side_rs.at[0]).wait_recv()
     for k in range(0, comps, chunk):
         cx = cxb[pl.ds(pl.multiple_of(me * comps + k, 16), chunk), :]
         px, mx = halves(cx)
-        from_east = edge_recv[0, 0, k:k + chunk].astype(F32)
-        from_west = edge_recv[0, 1, k:k + chunk].astype(F32)
+        from_east = side_recv[0, k:k + chunk].astype(F32)
+        from_west = side_recv[len(sides) - 1, k:k + chunk].astype(F32)
         for h in range(lines):
-            west_part = jnp.where(small % seg == 0, pltpu.roll(from_west, (width - h) % width, 1), 0.0)
+            west_part = jnp.where(small % seg == 0, pltpu.roll(from_west, (width - lines - h) % width, 1), 0.0)
             east_part = jnp.where(small % seg == seg - 1, pltpu.roll(from_east, seg - 1 - h, 1), 0.0)
             send_f[0, h, k:k + chunk] = (outer[0, h, k:k + chunk] + px * west_part).astype(BF16)
             send_f[blocks - 1, h, k:k + chunk] = (outer[1, h, k:k + chunk] + mx * east_part).astype(BF16)
@@ -440,14 +434,14 @@
             out.append(diff * diff)
         return out
 
-    def fresh_part(b, wind_rows, target, pair, quad):
+    def fresh_part(rows_of, wind_rows, target, pair, quad):
         outs = []
         for r in range(lines):
             cut = slice(r * width, (r + 1) * width)
-            f = cell_f[part(b), cut].astype(F32)
-            top = f + 0.3 * (f * pair[:, cut] - quad[:, cut]) + grow_b[part(b), :] * wind_rows[r]
+            f = cell_f[rows_of, cut].astype(F32)
+            top = f + 0.3 * (f * pair[:, cut] - quad[:, cut]) + grow_b[rows_of, :] * wind_rows[r]
             out = (sea[r] * (top / (1.0 + 0.1 * (f * f)))).astype(BF16)
-            target[part(b), cut] = out
+            target[rows_of, cut] = out
             outs.append(out)
         return outs
 
@@ -513,15 +507,16 @@
     for b in range(blocks):
         pair, quad = [total_v[i, part(b), :] + x
                       for i, x in enumerate(products(part(b), 1 - side))]
-        outs = fresh_part(b, wind_rows, e1, pair, quad)
+        outs = fresh_part(part(b), wind_rows, e1, pair, quad)
         for r in range(lines):
             slot = b * lines + r
             v = outs[r].astype(F32)
             first = jnp.where(lane % seg == slot, pltpu.roll(v, slot, 1), first)
             last = jnp.where(lane % seg == slot, pltpu.roll(v, (slot + 1 - seg) % width, 1), last)
-    edge_send[1, 0] = first.astype(BF16)
-    edge_send[1, 1] = last.astype(BF16)
-    send_edges(1)
+    edge_send[0] = first.astype(BF16)
+    edge_send[1] = last.astype(BF16)
+    for i, where in enumerate((near_west, near_east)):
+        remote(edge_send.at[i], edge_recv.at[i], edge_ss.at[0], edge_rs.at[0], where).start()
     release("edges", 6)
 
     west_rim = lane % seg == 0
@@ -548,9 +543,9 @@
     send_state(st1, 1)
     wind_rows = wind(st1)
 
-    whole(edge_recv.at[1], edge_rs.at[1]).wait_recv()
-    from_east = edge_recv[1, 0].astype(F32)
-    from_west = edge_recv[1, 1].astype(F32)
+    whole(edge_recv, edge_rs.at[0]).wait_recv()
+    from_east = edge_recv[0].astype(F32)
+    from_west = edge_recv[1].astype(F32)
     for b in range(blocks):
         px, mx = halves(cxb[part(b), :])
         for r in range(lines):
@@ -565,13 +560,24 @@
             wide = out.astype(F32)
             cell_s[part(b), cut] = (wide * wide).astype(BF16)
 
+    cuts = [(0, early.shape[0]), (early.shape[0], comps - early.shape[0])]
+
+    def send_back(b, q):
+        start, size = cuts[q]
+        remote(e2.at[pl.ds(pl.multiple_of(b * comps + start, 16), size), :], ret.at[spot, pl.ds(start, size), :],
+               ret_ss.at[0], ret_rs.at[q], block_id(b)).start()
+
     for b in order + [me]:
         weights = quartet_v[part(b), :]
         pair = jnp.dot(weights, cell_f[...], preferred_element_type=F32)
         quad = jnp.dot(weights, cell_s[...], preferred_element_type=F32)
-        fresh_part(b, wind_rows, e2, pair, quad)
+        outs = fresh_part(part(b), wind_rows, e2, pair, quad)
         if b is not me:
-            remote(e2.at[part(b), :], ret.at[spot], ret_ss.at[0], ret_rs.at[0], block_id(b)).start()
+            send_back(b, 0)
+    for r, out in enumerate(outs):
+        ret[spot, :, r * width:(r + 1) * width] = out
+    for b in order:
+        send_back(b, 1)
 
     whole(st_edge_recv.at[1], ste_rs.at[1]).wait_recv()
     update(st1, st2, 1, jnp.dot(coupler_v[...], e2[...], preferred_element_type=F32))
@@ -586,46 +592,48 @@
         core = lax.rem(b, lev_parts)
         remote(st_back.at[c, pl.ds(pl.multiple_of(core * lown, 16), lown), :], fin.at[spot], back_ss.at[0],
                back_rs.at[0], block_id(b)).start()
-    stores = [
-        pltpu.make_async_copy(st_back.at[mine_c, my_levels, :], fin.at[spot], own_sem.at[0]),
-        pltpu.make_async_copy(e2.at[part(me), :], ret.at[spot], own_sem.at[1]),
-    ]
-    for store in stores:
-        store.start()
-    whole(ret.at[others], ret_rs.at[0]).wait_recv()
+    fin[spot] = st_back[mine_c, my_levels, :]
+    for q, (start, size) in enumerate(cuts):
+        whole(ret.at[others, pl.ds(start, size), :], ret_rs.at[q]).wait_recv()
+        if q == 0:
+            to_rows(ret, early, flat, start)
     whole(fin.at[others], back_rs.at[0]).wait_recv()
 
     whole(send_f.at[others], f_send.at[0]).wait_send()
     whole(c_all.at[others], c_send.at[0]).wait_send()
     whole(swap_send.at[others], swap_ss.at[0]).wait_send()
     whole(sea_send.at[pl.ds(0, cell_tiles - 1)], sea_ss.at[0]).wait_send()
+    for _ in sides:
+        whole(side_send, side_ss.at[0]).wait_send()
     whole(edge_send, edge_ss.at[0]).wait_send()
     whole(st_edge_send, ste_ss.at[0]).wait_send()
     whole(ret.at[others], ret_ss.at[0]).wait_send()
     whole(fin.at[others], back_ss.at[0]).wait_send()
-    for store in stores:
-        store.wait()
-
-
-def unpack_kernel(ret, fin, spec_out, atm_out, oce_out, atm_v, oce_v, flat, spec_v, out_sem):
-    blocks, comps, cells = ret.shape
-    rows, width = spec_v.shape[1:]
-    lines = cells // width
-    seg = width // blocks
+
+
+def to_rows(ret, target, flat, start):
+    blocks = ret.shape[0]
+    size, rows, width = target.shape
+    lines = rows // blocks
+    for h in range(lines):
+        groups = swap_groups([
+            ret[t, start:start + size, h * width:(h + 1) * width].astype(F32) for t in range(blocks)
+        ], width // blocks)
+        for g, line in enumerate(groups):
+            flat[pl.ds(h * blocks + g, size, stride=rows), :] = line
+    target[...] = flat[pl.ds(0, size * rows), :].reshape(size, rows, width).astype(BF16)
+
+
+def unpack_kernel(ret, fin, early, spec_out, atm_out, oce_out, atm_v, oce_v, flat, late, out_sem):
+    blocks = ret.shape[0]
     tile_rows = atm_v.shape[1]
-    stores = []
-    for h in range(lines):
-        groups = swap_groups([ret[t, :, h * width:(h + 1) * width].astype(F32) for t in range(blocks)], seg)
-        for g, line in enumerate(groups):
-            flat[pl.ds(h * blocks + g, comps, stride=rows), :] = line
-    pieces = 3 if comps % 3 == 0 else 1
-    size = comps // pieces
-    for p in range(pieces):
-        cut = pl.ds(p * size, size)
-        spec_v[cut] = flat[pl.ds(p * size * rows, size * rows), :].reshape(size, rows, width).astype(BF16)
-        stores.append(pltpu.make_async_copy(spec_v.at[cut], spec_out.at[cut], out_sem.at[2 + p]))
-        stores[-1].start()
-    groups = swap_groups([fin[t].astype(F32) for t in range(blocks)], seg)
+    start = early.shape[0]
+    stores = [pltpu.make_async_copy(early, spec_out.at[pl.ds(0, start)], out_sem.at[2])]
+    stores[-1].start()
+    to_rows(ret, late, flat, start)
+    stores.append(pltpu.make_async_copy(late, spec_out.at[pl.ds(start, late.shape[0])], out_sem.at[3]))
+    stores[-1].start()
+    groups = swap_groups([fin[t].astype(F32) for t in range(blocks)], fin.shape[2] // blocks)
     for f, (target, out) in enumerate(((atm_v, atm_out), (oce_v, oce_out))):
         for r in range(tile_rows):
             target[:, r, :] = groups[f * tile_rows + r]
@@ -648,6 +656,7 @@
     lown, tile_rows, _ = atmosphere.shape
     levels = lown * lev_parts
     cells = lines * width
+    first = comps // 16 * 2 // 3 * 16
     depth = levels // (width // blocks // (2 * lines))
     v = pltpu.VMEM
     dma = pltpu.SemaphoreType.DMA
@@ -659,7 +668,7 @@
         v((blocks, lines, comps, width), BF16), v((total, cells), BF16), v((total, cells), BF16),
         v((blocks, 2, 1, comps), F32),
         v((total, width), F32), v((total, width), F32), v((total, width), F32),
-        v((NSTEP, 2, comps, width), BF16), v((NSTEP, 2, comps, width), BF16),
+        v((comps, width), BF16), v((2, comps, width), BF16), v((2, comps, width), BF16), v((2, comps, width), BF16),
         v((total, cells), BF16), v((total, cells), BF16),
         v((blocks, lown, width), BF16), v((cell_tiles, levels, width), BF16),
         v((blocks, 1, width), F32), v((cell_tiles, 1, width), F32),
@@ -669,21 +678,23 @@
         v((2, lines, levels, width), F32),
         v((NSTEP, 2, depth, width), F32), v((NSTEP, 2, depth, width), F32),
         v((cell_tiles, levels, width), BF16),
-        dma((9,)), dma((2,)), dma((1,)), dma((blocks,)), dma((1,)), dma((1,)),
-        dma((1,)), dma((NSTEP,)),
+        dma((9,)), dma((1,)), dma((blocks,)), dma((1,)), dma((1,)),
+        dma((1,)), dma((1,)), dma((1,)), dma((1,)),
         dma((1,)), dma((1,)), dma((1,)), dma((1,)),
         dma((1,)), dma((1,)),
         dma((1,)), dma((NSTEP,)),
-        dma((1,)), dma((1,)),
+        dma((1,)), dma((2,)),
     ]
     anywhere = pl.BlockSpec(memory_space=pltpu.HBM)
     here = pl.BlockSpec(memory_space=pltpu.VMEM)
     column = jax.ShapeDtypeStruct(atmosphere.shape, F32)
     packed = pl.pallas_call(
         functools.partial(fused_kernel, cell_tiles, lev_parts, sect_tiles),
-        out_shape=(v((blocks, comps, cells), BF16), v((blocks, lown, width), BF16)),
+        out_shape=(
+            v((blocks, comps, cells), BF16), v((blocks, lown, width), BF16), v((first, rows, width), BF16),
+        ),
         in_specs=[anywhere] * 9,
-        out_specs=(here,) * 2,
+        out_specs=(here,) * 3,
         scratch_shapes=scratch,
         compiler_params=pltpu.CompilerParams(
             collective_id=0, has_side_effects=True, vmem_limit_bytes=33554432
@@ -696,11 +707,11 @@
     return pl.pallas_call(
         unpack_kernel,
         out_shape=(jax.ShapeDtypeStruct(spectrum.shape, BF16), column, column),
-        in_specs=[here] * 2,
+        in_specs=[here] * 3,
         out_specs=(anywhere,) * 3,
         scratch_shapes=[
             v(atmosphere.shape, F32), v(atmosphere.shape, F32),
-            v((comps * rows, width), F32), v(spectrum.shape, BF16), dma((5,)),
+            v(((comps - first) * rows, width), F32), v((comps - first, rows, width), BF16), dma((4,)),
         ],
         compiler_params=pltpu.CompilerParams(vmem_limit_bytes=33554432),
     )(*packed)

time: 41.8 us -> 41.1 us (0.983)
  Pallas kernels: 41 us -> 40.3 us
    pallas_call x1, Pallas kernels: 1.99 us -> 1.2 us  [fused(): pl.pallas_call(unpack_kernel, out_shape=(jax.ShapeDtypeStruct(spectrum.sh...]
where the time goes in v4:
time: 41.1 us; the launch traced here: 41 us
  Pallas kernels  40.3 us (98%)
  between operations  0.64 us (2%)
    pallas_call x1, Pallas kernels, fused(): pl.pallas_call(functools.partial(fused_kernel, cell_tiles, lev_parts, sec...  39.1 us
    pallas_call x1, Pallas kernels, fused(): pl.pallas_call(unpack_kernel, out_shape=(jax.ShapeDtypeStruct(spectrum.sh...  1.2 us

profile of v4, /device:TPU:0, one launch (start us, length us, event | category | flops | bytes accessed | tf_op | source)
XLA Modules:
  0.0 41.0 jit_solution(15976838080029903213)
XLA Ops:
  0.6 39.1 %shard_map.112 = (bf16[8,144,256]{2,1,0:T(8,128)(2,1)S(1)}, bf16[8,32,128]{2,1,0:T(8,128)(2,1)S(1)}, bf16[96,16,128]{2,1,0:T(8,128)(2,1)S(1)}) custom-call(bf16[144,16,128]{2,1,0:T(8,128)(2,1)} %spec_hbm.1, f32[1,144]{1,0:T(1,128)} %bitcast.2, f32[1,144]{1,0:T(1,128)} %bitcast.3, f32[1152]{0:T(1024)} %growth_hbm.1, bf16[1152,1152]{1,0:T(8,128)(2,1)} %quartet_hbm.1, ...), custom_call_target="tpu_custom_call" | custom-call | tf_op jit(solution)/shard_map/pallas_call | solution.py:691
  39.8 1.2 %shard_map.113 = (bf16[144,16,128]{2,1,0:T(8,128)(2,1)}, f32[32,4,128]{2,1,0:T(4,128)}, f32[32,4,128]{2,1,0:T(4,128)}) custom-call(bf16[8,144,256]{2,1,0:T(8,128)(2,1)S(1)} %get-tuple-element.6.ret, bf16[8,32,128]{2,1,0:T(8,128)(2,1)S(1)} %get-tuple-element.7.fin, bf16[96,16,128]{2,1,0:T(8,128)(2,1)S(1)} %get-tuple-element.8.early), custom_call_target="tpu_custom_call" | custom-call | tf_op jit(solution)/shard_map/pallas_call | solution.py:707

commit v5 on v4

--- a/solution.py
+++ b/solution.py
@@ -10,6 +10,8 @@
 NSTEP = 2
 LANES = 128
 HELD = {6: {3: "edges", 2: "far"}}
+FIRST = (0, 4, 1, 5, 2, 3, 6)
+SECOND = (0, 4, 1, 5, 2, 3, 6)
 F32 = jnp.float32
 BF16 = jnp.bfloat16
 
@@ -144,8 +146,8 @@
 def fused_kernel(
     cell_tiles, lev_parts, sect_tiles,
     spec_hbm, cx_hbm, cy_hbm, growth_hbm, quartet_hbm, coupler_hbm, atm_hbm, oce_hbm, sea_hbm,
-    ret, fin, early,
-    spec_v, c_v, growth_v, quartet_v, coupler_v, col_in, sea_v,
+    ret, early, atm_v, oce_v,
+    spec_v, fin, c_v, growth_v, quartet_v, coupler_v, col_in, sea_v,
     flat, rows_v, send_f, cell_f, cell_s, c_all, cxb, cyb, grow_b,
     side_send, side_recv, edge_send, edge_recv, e1, e2,
     swap_send, st_in, sea_send, sea_in, outer, inner, stage_v, total_v, st0, st1, st2, st_edge_send, st_edge_recv, st_back,
@@ -567,7 +569,7 @@
         remote(e2.at[pl.ds(pl.multiple_of(b * comps + start, 16), size), :], ret.at[spot, pl.ds(start, size), :],
                ret_ss.at[0], ret_rs.at[q], block_id(b)).start()
 
-    for b in order + [me]:
+    for b in [order[i] for i in FIRST] + [me]:
         weights = quartet_v[part(b), :]
         pair = jnp.dot(weights, cell_f[...], preferred_element_type=F32)
         quad = jnp.dot(weights, cell_s[...], preferred_element_type=F32)
@@ -576,9 +578,6 @@
             send_back(b, 0)
     for r, out in enumerate(outs):
         ret[spot, :, r * width:(r + 1) * width] = out
-    for b in order:
-        send_back(b, 1)
-
     whole(st_edge_recv.at[1], ste_rs.at[1]).wait_recv()
     update(st1, st2, 1, jnp.dot(coupler_v[...], e2[...], preferred_element_type=F32))
     for h in range(lines):
@@ -593,11 +592,16 @@
         remote(st_back.at[c, pl.ds(pl.multiple_of(core * lown, 16), lown), :], fin.at[spot], back_ss.at[0],
                back_rs.at[0], block_id(b)).start()
     fin[spot] = st_back[mine_c, my_levels, :]
-    for q, (start, size) in enumerate(cuts):
-        whole(ret.at[others, pl.ds(start, size), :], ret_rs.at[q]).wait_recv()
-        if q == 0:
-            to_rows(ret, early, flat, start)
+    for b in [order[i] for i in SECOND]:
+        send_back(b, 1)
+    whole(ret.at[others, pl.ds(0, cuts[0][1]), :], ret_rs.at[0]).wait_recv()
+    to_rows(ret, early, flat, 0)
     whole(fin.at[others], back_rs.at[0]).wait_recv()
+    groups = swap_groups([fin[t].astype(F32) for t in range(blocks)], seg)
+    for f, target in enumerate((atm_v, oce_v)):
+        for r in range(tile_rows):
+            target[:, r, :] = groups[f * tile_rows + r]
+    whole(ret.at[others, pl.ds(*cuts[1]), :], ret_rs.at[1]).wait_recv()
 
     whole(send_f.at[others], f_send.at[0]).wait_send()
     whole(c_all.at[others], c_send.at[0]).wait_send()
@@ -624,21 +628,17 @@
     target[...] = flat[pl.ds(0, size * rows), :].reshape(size, rows, width).astype(BF16)
 
 
-def unpack_kernel(ret, fin, early, spec_out, atm_out, oce_out, atm_v, oce_v, flat, late, out_sem):
-    blocks = ret.shape[0]
-    tile_rows = atm_v.shape[1]
+def unpack_kernel(ret, early, atm_v, oce_v, spec_out, atm_out, oce_out, flat, late, out_sem):
     start = early.shape[0]
-    stores = [pltpu.make_async_copy(early, spec_out.at[pl.ds(0, start)], out_sem.at[2])]
-    stores[-1].start()
+    stores = [
+        pltpu.make_async_copy(x, y, out_sem.at[i])
+        for i, (x, y) in enumerate(((early, spec_out.at[pl.ds(0, start)]), (atm_v, atm_out), (oce_v, oce_out)))
+    ]
+    for store in stores:
+        store.start()
     to_rows(ret, late, flat, start)
     stores.append(pltpu.make_async_copy(late, spec_out.at[pl.ds(start, late.shape[0])], out_sem.at[3]))
     stores[-1].start()
-    groups = swap_groups([fin[t].astype(F32) for t in range(blocks)], fin.shape[2] // blocks)
-    for f, (target, out) in enumerate(((atm_v, atm_out), (oce_v, oce_out))):
-        for r in range(tile_rows):
-            target[:, r, :] = groups[f * tile_rows + r]
-        stores.append(pltpu.make_async_copy(target, out, out_sem.at[f]))
-        stores[-1].start()
     for store in stores:
         store.wait()
 
@@ -661,7 +661,7 @@
     v = pltpu.VMEM
     dma = pltpu.SemaphoreType.DMA
     scratch = [
-        v((comps, rows, width), BF16), v((2, 1, comps), F32),
+        v((comps, rows, width), BF16), v((blocks, lown, width), BF16), v((2, 1, comps), F32),
         v((total,), F32), v((total, total), BF16), v(coupler.shape, BF16),
         v((2, lown, tile_rows, width), F32), v(sea_mask.shape, jnp.int32),
         v((comps * rows, width), F32), v((rows, comps, width), F32),
@@ -691,10 +691,11 @@
     packed = pl.pallas_call(
         functools.partial(fused_kernel, cell_tiles, lev_parts, sect_tiles),
         out_shape=(
-            v((blocks, comps, cells), BF16), v((blocks, lown, width), BF16), v((first, rows, width), BF16),
+            v((blocks, comps, cells), BF16), v((first, rows, width), BF16),
+            v(atmosphere.shape, F32), v(atmosphere.shape, F32),
         ),
         in_specs=[anywhere] * 9,
-        out_specs=(here,) * 3,
+        out_specs=(here,) * 4,
         scratch_shapes=scratch,
         compiler_params=pltpu.CompilerParams(
             collective_id=0, has_side_effects=True, vmem_limit_bytes=33554432
@@ -707,10 +708,9 @@
     return pl.pallas_call(
         unpack_kernel,
         out_shape=(jax.ShapeDtypeStruct(spectrum.shape, BF16), column, column),
-        in_specs=[here] * 3,
+        in_specs=[here] * 4,
         out_specs=(anywhere,) * 3,
         scratch_shapes=[
-            v(atmosphere.shape, F32), v(atmosphere.shape, F32),
             v(((comps - first) * rows, width), F32), v((comps - first, rows, width), BF16), dma((4,)),
         ],
         compiler_params=pltpu.CompilerParams(vmem_limit_bytes=33554432),

time: 41.1 us -> 40.2 us (0.978)
  Pallas kernels: 40.3 us -> 39.4 us
    pallas_call x1, Pallas kernels: 39.1 us -> 38.2 us  [fused(): pl.pallas_call(functools.partial(fused_kernel, cell_tiles, lev_parts, sec...]
where the time goes in v5:
time: 40.2 us; the launch traced here: 40 us
  Pallas kernels  39.4 us (98%)
  between operations  0.64 us (2%)
    pallas_call x1, Pallas kernels, fused(): pl.pallas_call(functools.partial(fused_kernel, cell_tiles, lev_parts, sec...  38.2 us
    pallas_call x1, Pallas kernels, fused(): pl.pallas_call(unpack_kernel, out_shape=(jax.ShapeDtypeStruct(spectrum.sh...  1.16 us

profile of v5, /device:TPU:0, one launch (start us, length us, event | category | flops | bytes accessed | tf_op | source)
XLA Modules:
  0.0 40.0 jit_solution(1961302754467092384)
XLA Ops:
  0.6 38.2 %shard_map.112 = (bf16[8,144,256]{2,1,0:T(8,128)(2,1)S(1)}, bf16[96,16,128]{2,1,0:T(8,128)(2,1)S(1)}, f32[32,4,128]{2,1,0:T(4,128)S(1)}, f32[32,4,128]{2,1,0:T(4,128)S(1)}) custom-call(bf16[144,16,128]{2,1,0:T(8,128)(2,1)} %spec_hbm.1, f32[1,144]{1,0:T(1,128)} %bitcast.2, f32[1,144]{1,0:T(1,128)} %bitcast.3, f32[1152]{0:T(1024)} %growth_hbm.1, ...), custom_call_target="tpu_custom_call" | custom-call | tf_op jit(solution)/shard_map/pallas_call | solution.py:691
  38.9 1.2 %shard_map.113 = (bf16[144,16,128]{2,1,0:T(8,128)(2,1)}, f32[32,4,128]{2,1,0:T(4,128)}, f32[32,4,128]{2,1,0:T(4,128)}) custom-call(bf16[8,144,256]{2,1,0:T(8,128)(2,1)S(1)} %get-tuple-element.7.ret, bf16[96,16,128]{2,1,0:T(8,128)(2,1)S(1)} %get-tuple-element.8.early, f32[32,4,128]{2,1,0:T(4,128)S(1)} %get-tuple-element.9.atm_v, ...), custom_call_target="tpu_custom_call" | custom-call | tf_op jit(solution)/shard_map/pallas_call | solution.py:708

commit v6 on v5

--- a/solution.py
+++ b/solution.py
@@ -10,7 +10,7 @@
 NSTEP = 2
 LANES = 128
 HELD = {6: {3: "edges", 2: "far"}}
-FIRST = (0, 4, 1, 5, 2, 3, 6)
+FIRST = (2, 4, 0, 5, 1, 3, 6)
 SECOND = (0, 4, 1, 5, 2, 3, 6)
 F32 = jnp.float32
 BF16 = jnp.bfloat16
@@ -512,9 +512,9 @@
         outs = fresh_part(part(b), wind_rows, e1, pair, quad)
         for r in range(lines):
             slot = b * lines + r
-            v = outs[r].astype(F32)
-            first = jnp.where(lane % seg == slot, pltpu.roll(v, slot, 1), first)
-            last = jnp.where(lane % seg == slot, pltpu.roll(v, (slot + 1 - seg) % width, 1), last)
+            v = pltpu.roll(outs[r].astype(F32), slot, 1)
+            first = jnp.where(lane % seg == slot, v, first)
+            last = jnp.where(lane % seg == (slot + seg - 1) % seg, v, last)
     edge_send[0] = first.astype(BF16)
     edge_send[1] = last.astype(BF16)
     for i, where in enumerate((near_west, near_east)):
@@ -554,7 +554,7 @@
             slot = b * lines + r
             cut = slice(r * width, (r + 1) * width)
             beside = jnp.where(
-                west_rim, px * pltpu.roll(from_west, (width - slot) % width, 1),
+                west_rim, px * pltpu.roll(from_west, (width - slot - seg + 1) % width, 1),
                 mx * pltpu.roll(from_east, (width + seg - 1 - slot) % width, 1),
             )
             out = (inner[part(b), cut] + jnp.where(west_rim | east_rim, beside, 0.0)).astype(BF16)

time: 40.2 us -> 40.2 us (level)
  no operation moved by 1% of the time
where the time goes in v6:
time: 40.2 us; the launch traced here: 40 us
  Pallas kernels  39.4 us (98%)
  between operations  0.64 us (2%)
    pallas_call x1, Pallas kernels, fused(): pl.pallas_call(functools.partial(fused_kernel, cell_tiles, lev_parts, sec...  38.2 us
    pallas_call x1, Pallas kernels, fused(): pl.pallas_call(unpack_kernel, out_shape=(jax.ShapeDtypeStruct(spectrum.sh...  1.16 us

profile of v6, /device:TPU:0, one launch (start us, length us, event | category | flops | bytes accessed | tf_op | source)
XLA Modules:
  0.0 40.0 jit_solution(13331030799932105560)
XLA Ops:
  0.6 38.2 %shard_map.112 = (bf16[8,144,256]{2,1,0:T(8,128)(2,1)S(1)}, bf16[96,16,128]{2,1,0:T(8,128)(2,1)S(1)}, f32[32,4,128]{2,1,0:T(4,128)S(1)}, f32[32,4,128]{2,1,0:T(4,128)S(1)}) custom-call(bf16[144,16,128]{2,1,0:T(8,128)(2,1)} %spec_hbm.1, f32[1,144]{1,0:T(1,128)} %bitcast.2, f32[1,144]{1,0:T(1,128)} %bitcast.3, f32[1152]{0:T(1024)} %growth_hbm.1, ...), custom_call_target="tpu_custom_call" | custom-call | tf_op jit(solution)/shard_map/pallas_call | solution.py:691
  38.9 1.2 %shard_map.113 = (bf16[144,16,128]{2,1,0:T(8,128)(2,1)}, f32[32,4,128]{2,1,0:T(4,128)}, f32[32,4,128]{2,1,0:T(4,128)}) custom-call(bf16[8,144,256]{2,1,0:T(8,128)(2,1)S(1)} %get-tuple-element.7.ret, bf16[96,16,128]{2,1,0:T(8,128)(2,1)S(1)} %get-tuple-element.8.early, f32[32,4,128]{2,1,0:T(4,128)S(1)} %get-tuple-element.9.atm_v, ...), custom_call_target="tpu_custom_call" | custom-call | tf_op jit(solution)/shard_map/pallas_call | solution.py:708
